TPU v7x, 32 devices: a whole 2x2x4 slice. The times are simulated.
32 devices in a mesh: ax: 8 (over z, x), rad: 4 (over y, core).
Axes of the slice: x: 2, y: 2, z: 4, core: 2. Of those that a mesh axis runs over, the one named last changes fastest.
Arguments:
- velocity: float32 [3, 12, 24, 768], P(None, 'rad', 'ax'), may hold values from -50 to 50
- cycle_map: int32 [3, 768], replicated, may hold values from 0 to 95, never falling along the last dimension, each value on 1 to 16 neighbouring positions
Outputs:
- new_velocity: float32 [3, 12, 24, 768], P(None, 'rad', 'ax')
Inputs may be any that keep to these rules, and one draw needn't show every extreme that they name: `cycle_map`: in each row the numbers never fall along the azimuth, and each of 0 to 95 is taken by 1 to 16 consecutive points, one by exactly 16.
All inputs are finite; a program needn't handle non-finite values.
Results may differ from a plain program's by a relative error of at most 0.0003.
Values sent between devices are 32-bit elements; how exact they have to be, the bound alone decides.
A program may use at most 64 MiB of HBM per device.

v0:
```python
import functools

import jax
import jax.numpy as jnp
from jax import lax
from jax.experimental import pallas as pl
from jax.experimental.pallas import tpu as pltpu
from jax.sharding import PartitionSpec as P

NRING = 3
MOSTSEG = 16
SUB = 8
LANES = 128
PAIRS = ((0, 0), (1, 1), (2, 2), (0, 1), (0, 2), (1, 2))
PAIR_WEIGHTS = (1.0, 1.0, 1.0, 2.0, 2.0, 2.0)
SIGNS = (1.0, -1.0, -1.0)
EPSILON = 1e-06
MESH = pl.DeviceIdType.MESH


def pair(a, b):
    return PAIRS.index((min(a, b), max(a, b)))


def each(count, body):
    if count <= 16:
        for i in range(count):
            body(i)
    else:
        lax.fori_loop(0, count, lambda i, c: (body(i), c)[1], 0)


def roll(x, shift, axis):
    size = x.shape[axis]
    return pltpu.roll(x, shift % size, axis)


def up(x):
    return roll(x, -1, x.ndim - 1)


def down(x):
    return roll(x, 1, x.ndim - 1)


def smooth_t(x):
    return (down(x) + 2.0 * x + up(x)) * 0.25


def smooth_z(x):
    return (x[:, :-2] + 2.0 * x[:, 1:-1] + x[:, 2:]) * 0.25


def tiles_of(x):
    return [x[:, k : k + LANES] for k in range(0, x.shape[1], LANES)]


def segments(x, wide, pad):
    rows, tiles = x[0].shape[0], len(x)
    total = tiles * LANES
    lane = lax.broadcasted_iota(jnp.int32, (rows, LANES), 1)
    pieces = []
    for s in range(SUB):
        start = (s * wide - pad) % total
        k, off = start // LANES, start % LANES
        first = x[k]
        if off:
            k2 = (k + 1) % tiles
            second = x[k2]
            first = jnp.where(lane < LANES - off, roll(first, -off, 1), roll(second, -off, 1))
        pieces.append(first)
    return pieces


def joined(pieces, wide, pad):
    rows = pieces[0].shape[0]
    lane = lax.broadcasted_iota(jnp.int32, (rows, LANES), 1)
    tiles = []
    for k in range(SUB * wide // LANES):
        lo, hi = k * LANES, (k + 1) * LANES
        s = lo // wide
        out = None
        while s * wide < hi:
            part = roll(pieces[s], s * wide - pad - lo, 1)
            out = part if out is None else jnp.where(lane >= s * wide - lo, part, out)
            s += 1
        tiles.append(out)
    return tiles


def strain(grads):
    tensor = []
    for c, a in PAIRS:
        if c == a:
            tensor.append(0.5 * grads[c][c])
        else:
            tensor.append(0.25 * (grads[c][a] + grads[a][c]))
    squares = sum(w * m * m for w, m in zip(PAIR_WEIGHTS, tensor))
    return tensor, jnp.sqrt(2.0 * squares)


def gradients(f):
    out = []
    for c in range(3):
        mid = f[c][1:-1, 1:-1]
        out.append(
            [
                f[c][1:-1, 2:] - f[c][1:-1, :-2],
                f[c][2:, 1:-1] - f[c][:-2, 1:-1],
                up(mid) - down(mid),
            ]
        )
    return out


def stages(n_ax):
    distances, own, beside = [1], 2, 1
    while own < n_ax // 2:
        distances.append(own)
        own, beside = 2 * own, beside + own
    while beside < n_ax // 2:
        distances.append(1)
        beside += 1
    return distances


def kernel(n_ax, n_rad, v_hbm, map_hbm, out_ref, nat, map_ref, own, maps, ext, hx, part, parts, edge_coef,
           z_out, z_in, z_seg, ready, in_sems, halo_send, halo_recv, h_send, h_recv, p_send, p_recv):
    rad = lax.axis_index("rad")
    ax = lax.axis_index("ax")
    R, Z, T = nat.shape[1], nat.shape[2], nat.shape[3]
    wide = T // SUB
    pad = (LANES - wide) // 2
    half = SUB // 2
    right, left = lax.rem(ax + 1, n_ax), lax.rem(ax + n_ax - 1, n_ax)
    has_lo, has_hi = rad > 0, rad < n_rad - 1

    def strips(c, r):
        return [own[pl.ds((c * R + r) * Z * SUB + s, Z, stride=SUB), :] for s in range(SUB)]

    barrier = pltpu.get_barrier_semaphore()

    def greet(to_ax, to_rad):
        pl.semaphore_signal(barrier, inc=1, device_id=(to_ax, to_rad), device_id_type=MESH)

    greet(left, rad)
    greet(right, rad)
    pl.when(has_lo)(lambda: greet(ax, rad - 1))
    pl.when(has_hi)(lambda: greet(ax, rad + 1))

    distances = stages(n_ax)

    def tell(stage):
        d = distances[stage]
        for peer in (lax.rem(ax + d, n_ax), lax.rem(ax + n_ax - d, n_ax)):
            pl.semaphore_signal(ready.at[stage], inc=1, device_id=(peer, rad), device_id_type=MESH)

    def hear(stage):
        pl.semaphore_wait(ready.at[stage], 2)

    fetch = pltpu.make_async_copy(v_hbm, nat, in_sems.at[0])
    fetch.start()
    fetch_map = pltpu.make_async_copy(map_hbm, map_ref, in_sems.at[1])
    pl.when(rad == 0)(lambda: fetch_map.start())
    fetch.wait()
    for c in range(3):
        for r in range(R):
            for s, piece in enumerate(segments(tiles_of(nat[c, r]), wide, pad)):
                own[pl.ds((c * R + r) * Z * SUB + s, Z, stride=SUB), :] = piece
    for c in range(3):
        for r in range(R):
            for z in range(Z):
                row = ((c * R + r) * Z + z) * SUB
                ext[c, r + 1, z + 2] = own[row : row + SUB, :]

    lane = lax.broadcasted_iota(jnp.int32, (SUB, LANES), 1)
    steps = []
    while 2 ** len(steps) < MOSTSEG:
        steps.append(2 ** len(steps))

    def cell_sums(r):
        label = maps[r * SUB : (r + 1) * SUB, :]
        before = [(roll(label, d, 1) == label).astype(jnp.float32) for d in steps]
        after = [(roll(label, -d, 1) == label).astype(jnp.float32) for d in steps]

        def spread(x):
            total, rest = x, x
            for d, b, a in zip(steps, before, after):
                total = total + b * roll(total, d, 1)
                rest = rest + a * roll(rest, -d, 1)
            return total + rest - x

        return spread

    def coarsen(r, spread, c, z):
        mean = spread(ext[c, r + 1, z]) * maps[(NRING + r) * SUB : (NRING + r + 1) * SUB, :]
        low = roll(roll(mean, -wide, 1), 1, 0)
        high = roll(roll(mean, wide, 1), -1, 0)
        mean = jnp.where(lane < pad, low, mean)
        ext[c, r + 1, z] = jnp.where(lane >= pad + wide, high, mean)

    @pl.when(rad == 0)
    def _():
        fetch_map.wait()
        labels = map_ref[...].astype(jnp.float32)
        for s, piece in enumerate(segments(tiles_of(labels), wide, pad)):
            maps[pl.ds(s, NRING, stride=SUB), :] = piece
        for r in range(NRING):
            spread = cell_sums(r)
            maps[(NRING + r) * SUB : (NRING + r + 1) * SUB, :] = 1.0 / spread(jnp.ones((SUB, LANES), jnp.float32))
            for c in range(3):
                for z in range(Z):
                    coarsen(r, spread, c, z + 2)
                    row = ((c * R + r) * Z + z) * SUB
                    own[row : row + SUB, :] = ext[c, r + 1, z + 2]
                for k, tile in enumerate(joined(strips(c, r), wide, pad)):
                    nat[c, r, :, k * LANES : (k + 1) * LANES] = tile

    n_rows = 3 * R * 2
    for side, first in ((0, Z - 2), (1, 0)):
        for c in range(3):
            for r in range(R):
                for k in range(T // LANES):
                    row = k * n_rows + (c * R + r) * 2
                    z_out[side, row : row + 2, :] = nat[c, r, first : first + 2, k * LANES : (k + 1) * LANES]

    pl.semaphore_wait(barrier, 2 + jnp.where(has_lo, 1, 0) + jnp.where(has_hi, 1, 0))

    def z_halo(slot, to_ax):
        return pltpu.make_async_remote_copy(
            src_ref=z_out.at[slot], dst_ref=z_in.at[slot], send_sem=halo_send.at[slot],
            recv_sem=halo_recv.at[slot], device_id=(to_ax, rad), device_id_type=MESH)

    z_lo, z_hi = z_halo(0, right), z_halo(1, left)
    z_lo.start()
    z_hi.start()
    tell(0)

    rows, cols = pl.ds(1, R), pl.ds(2, Z)

    def halo(slot, src, dst, to_ax, to_rad):
        return pltpu.make_async_remote_copy(
            src_ref=ext.at[src], dst_ref=ext.at[dst], send_sem=halo_send.at[slot],
            recv_sem=halo_recv.at[slot], device_id=(to_ax, to_rad), device_id_type=MESH)

    everything = slice(None)

    out_going = [
        halo(2, (everything, R, cols), (everything, 0, cols), ax, rad + 1),
        halo(3, (everything, R, Z + 1), (everything, 0, 1), right, rad + 1),
        halo(4, (everything, R, 2), (everything, 0, Z + 2), left, rad + 1),
    ]
    in_going = [
        halo(5, (everything, 1, cols), (everything, R + 1, cols), ax, rad - 1),
        halo(6, (everything, 1, Z + 1), (everything, R + 1, 1), right, rad - 1),
        halo(7, (everything, 1, 2), (everything, R + 1, Z + 2), left, rad - 1),
    ]

    def start_all(copies):
        for copy in copies:
            copy.start()

    def wait_recv(copies):
        for copy in copies:
            copy.wait_recv()

    def wait_send(copies):
        for copy in copies:
            copy.wait_send()

    pl.when(has_hi)(lambda: start_all(out_going[:1]))
    pl.when(has_lo)(lambda: start_all(in_going[:1]))
    for stage in range(len(distances) - 1)[:1]:
        hear(stage)
        tell(stage + 1)
    pl.when(has_hi)(lambda: start_all(out_going[1:]))
    pl.when(has_lo)(lambda: start_all(in_going[1:]))
    for side, copy, first in ((0, z_lo, 0), (1, z_hi, Z + 2)):
        copy.wait_recv()
        tiles = [z_in[side, k * n_rows : (k + 1) * n_rows, :] for k in range(T // LANES)]
        for s, piece in enumerate(segments(tiles, wide, pad)):
            z_seg[pl.ds(side * n_rows * SUB + s, n_rows, stride=SUB), :] = piece
        for c in range(3):
            for r in range(R):
                for z in range(2):
                    row = (side * n_rows + (c * R + r) * 2 + z) * SUB
                    ext[c, r + 1, first + z] = z_seg[row : row + SUB, :]
    for stage in range(1, len(distances) - 1):
        hear(stage)
        tell(stage + 1)

    long = [ext[c, 1 : R + 1, 0 : Z + 4] for c in range(3)]
    mids = [x[:, 1:-1] for x in long]
    grads, w_own, w_grads, leonards = [], [], [], []
    for c in range(3):
        turned = up(mids[c]) - down(mids[c])
        grads.append([long[c][:, 2:] - long[c][:, :-2], None, turned])
        w_own.append(smooth_t(smooth_z(long[c])))
        mid = w_own[c][:, 1:-1]
        w_grads.append([w_own[c][:, 2:] - w_own[c][:, :-2], None, up(mid) - down(mid)])
    for c, a in PAIRS:
        product = smooth_t(smooth_z(mids[c] * mids[a]))
        leonards.append(product - w_own[c][:, 1:-1] * w_own[a][:, 1:-1])

    pl.when(has_lo)(lambda: wait_recv(out_going))
    pl.when(has_hi)(lambda: wait_recv(in_going))

    @pl.when(rad == 0)
    def _():
        for c in range(3):
            for z in range(1, Z + 3):
                ext[c, 0, z] = SIGNS[c] * roll(ext[c, 1, z], half, 0)

    @pl.when(rad == n_rad - 1)
    def _():
        for c in range(3):
            for z in range(1, Z + 3):
                ext[c, R + 1, z] = jnp.zeros((SUB, LANES), jnp.float32)

    below = [ext[c, 0:1, 1 : Z + 3] for c in range(3)]
    above = [ext[c, R + 1 : R + 2, 1 : Z + 3] for c in range(3)]
    for c in range(3):
        column = jnp.concatenate([below[c], mids[c], above[c]], axis=0)
        grads[c][1] = column[2:] - column[:-2]
        column = jnp.concatenate(
            [smooth_t(smooth_z(below[c])), w_own[c][:, 1:-1], smooth_t(smooth_z(above[c]))], axis=0)
        w_grads[c][1] = column[2:] - column[:-2]
    tensor, mag = strain(grads)
    stress = [mag * t for t in tensor]
    w_tensor, w_mag = strain(w_grads)
    w_mag4 = 4.0 * w_mag
    lm, mm = 0.0, 0.0
    for number, leonard in enumerate(leonards):
        model = smooth_t(smooth_z(stress[number])) - w_mag4 * w_tensor[number]
        lm = lm + PAIR_WEIGHTS[number] * leonard * model
        mm = mm + PAIR_WEIGHTS[number] * model * model
    sub_index = lax.broadcasted_iota(jnp.int32, (SUB, LANES), 0)
    lane_index = lax.broadcasted_iota(jnp.int32, (SUB, LANES), 1)
    mine = jnp.zeros((SUB, LANES), jnp.float32)
    for r in range(R):
        for base, quantity in ((0, lm), (half, mm)):
            row = jnp.sum(jnp.sum(quantity[r], axis=0), axis=0, keepdims=True)
            mine = jnp.where(sub_index == base + r, row, mine)
    mine = jnp.where((lane_index >= pad) & (lane_index < pad + wide), mine, 0.0)
    fold = LANES // 2
    while fold >= LANES // SUB:
        mine = mine + roll(mine, fold, 1)
        fold //= 2
    group = lane_index // (LANES // SUB) == sub_index
    part[...] = jnp.sum(jnp.where(group, mine, 0.0), axis=0, keepdims=True)

    def sums(side, i):
        peer = lax.rem(ax + i, n_ax)
        return pltpu.make_async_remote_copy(
            src_ref=part, dst_ref=parts.at[(1 - side) * n_ax + ax],
            send_sem=p_send.at[(1 + side) * n_ax + i], recv_sem=p_recv.at[(1 - side) * n_ax + ax],
            device_id=(peer, rad + side), device_id_type=MESH)

    def sums_in(side, i):
        peer = lax.rem(ax + i, n_ax)
        slot = (1 + side) * n_ax + peer
        return pltpu.make_async_remote_copy(
            src_ref=part, dst_ref=parts.at[slot],
            send_sem=p_send.at[(1 + side) * n_ax + i], recv_sem=p_recv.at[slot],
            device_id=(peer, rad + side), device_id_type=MESH)

    def first_of(side):
        return 1 if side == 0 else 0

    def send_sums(side):
        first = first_of(side)
        each(n_ax - first, lambda i: sums(side, i + first).start())

    send_sums(0)
    hear(len(distances) - 1)
    pl.when(has_lo)(lambda: send_sums(-1))
    pl.when(has_hi)(lambda: send_sums(1))

    for c in range(3):
        hx[c, 1 : R + 1] = stress[pair(c, 1)][:, 1:-1]

    def edge(slot, src, dst, to_rad):
        return pltpu.make_async_remote_copy(
            src_ref=hx.at[:, src], dst_ref=hx.at[:, dst], send_sem=h_send.at[slot],
            recv_sem=h_recv.at[slot], device_id=(ax, to_rad), device_id_type=MESH)

    edge_out = edge(0, R, 0, rad + 1)
    edge_in = edge(1, 1, R + 1, rad - 1)
    pl.when(has_hi)(lambda: edge_out.start())
    pl.when(has_lo)(lambda: edge_in.start())

    @pl.when(rad == 0)
    def _():
        for c in range(3):
            for z in range(Z):
                hx[c, 0, z] = SIGNS[c] * SIGNS[1] * roll(hx[c, 1, z], half, 0)

    @pl.when(rad == n_rad - 1)
    def _():
        for c in range(3):
            for z in range(Z):
                hx[c, R + 1, z] = jnp.zeros((SUB, LANES), jnp.float32)

    bases, turns = [], []
    whole = [jnp.concatenate([below[c], mids[c], above[c]], axis=0)[:, 1:-1] for c in range(3)]
    for c in range(3):
        axial = mids[c] * mids[0]
        radial = whole[c] * whole[1]
        around = whole[c][1:-1] * whole[2][1:-1]
        change = axial[:, 2:] - axial[:, :-2] + (radial[2:] - radial[:-2]) + (up(around) - down(around))
        bases.append(whole[c][1:-1] - 0.5 * change)
        along = stress[pair(c, 0)]
        turn = stress[pair(c, 2)][:, 1:-1]
        turns.append(along[:, 2:] - along[:, :-2] + (up(turn) - down(turn)))

    count = n_ax * Z * T
    each(n_ax - 1, lambda i: sums_in(0, i + 1).wait_recv())

    def coefficients(total):
        total = jnp.broadcast_to(jnp.sum(jnp.where(group, total, 0.0), axis=1, keepdims=True), (SUB, LANES)) / count
        return total / (roll(total, -half, 0) + EPSILON)

    def total_of(side):
        first = first_of(side)
        total = part[...] if first else jnp.zeros((1, LANES), jnp.float32)
        if n_ax <= 16:
            for i in range(first, n_ax):
                total = total + parts[(1 + side) * n_ax + lax.rem(ax + i, n_ax)]
            return total
        return lax.fori_loop(
            first, n_ax, lambda i, t: t + parts[(1 + side) * n_ax + lax.rem(ax + i, n_ax)], total)

    coef = coefficients(total_of(0))

    def beside(side, row):
        each(n_ax, lambda i: sums_in(side, i).wait_recv())
        edge_coef[0 if side < 0 else 1] = jnp.broadcast_to(
            coefficients(total_of(side))[row : row + 1], (SUB, LANES))

    pl.when(has_lo)(lambda: beside(-1, R - 1))
    pl.when(has_hi)(lambda: beside(1, 0))

    @pl.when(rad == 0)
    def _():
        edge_coef[0] = jnp.broadcast_to(coef[0:1], (SUB, LANES))

    @pl.when(rad == n_rad - 1)
    def _():
        edge_coef[1] = jnp.zeros((SUB, LANES), jnp.float32)

    pl.when(has_lo)(lambda: edge_out.wait_recv())
    pl.when(has_hi)(lambda: edge_in.wait_recv())
    by_row = [edge_coef[0]] + [jnp.broadcast_to(coef[r : r + 1], (SUB, LANES)) for r in range(R)] + [edge_coef[1]]
    for c in range(3):
        for r in range(R):
            new = bases[c][r] + by_row[r + 1] * turns[c][r]
            new = new + (by_row[r + 2] * hx[c, r + 2] - by_row[r] * hx[c, r])
            for z in range(Z):
                row = ((c * R + r) * Z + z) * SUB
                own[row : row + SUB, :] = new[z]
    for c in range(3):
        for r in range(R):
            for k, tile in enumerate(joined(strips(c, r), wide, pad)):
                out_ref[c, r, :, k * LANES : (k + 1) * LANES] = tile

    wait_send([z_lo, z_hi])

    @pl.when(has_hi)
    def _():
        wait_send(out_going + [edge_out])
        each(n_ax, lambda i: sums(1, i).wait_send())

    @pl.when(has_lo)
    def _():
        wait_send(in_going + [edge_in])
        each(n_ax, lambda i: sums(-1, i).wait_send())

    each(n_ax - 1, lambda i: sums(0, i + 1).wait_send())


def shards(n_ax, n_rad, velocity, cycle_map):
    _, R, Z, T = velocity.shape
    return pl.pallas_call(
        functools.partial(kernel, n_ax, n_rad),
        out_shape=jax.ShapeDtypeStruct(velocity.shape, velocity.dtype),
        in_specs=[pl.BlockSpec(memory_space=pltpu.HBM)] * 2,
        out_specs=pl.BlockSpec(memory_space=pltpu.VMEM),
        scratch_shapes=[
            pltpu.VMEM(velocity.shape, jnp.float32),
            pltpu.VMEM(cycle_map.shape, jnp.int32),
            pltpu.VMEM((3 * R * Z * SUB, LANES), jnp.float32),
            pltpu.VMEM((2 * NRING * SUB, LANES), jnp.float32),
            pltpu.VMEM((3, R + 2, Z + 4, SUB, LANES), jnp.float32),
            pltpu.VMEM((3, R + 2, Z, SUB, LANES), jnp.float32),
            pltpu.VMEM((1, LANES), jnp.float32),
            pltpu.VMEM((3 * n_ax, 1, LANES), jnp.float32),
            pltpu.VMEM((2, SUB, LANES), jnp.float32),
            pltpu.VMEM((2, 3 * R * 2 * T // LANES, LANES), jnp.float32),
            pltpu.VMEM((2, 3 * R * 2 * T // LANES, LANES), jnp.float32),
            pltpu.VMEM((2 * 3 * R * 2 * SUB, LANES), jnp.float32),
            pltpu.SemaphoreType.REGULAR((len(stages(n_ax)),)),
            pltpu.SemaphoreType.DMA((2,)),
            pltpu.SemaphoreType.DMA((8,)),
            pltpu.SemaphoreType.DMA((8,)),
            pltpu.SemaphoreType.DMA((2,)),
            pltpu.SemaphoreType.DMA((2,)),
            pltpu.SemaphoreType.DMA((3 * n_ax,)),
            pltpu.SemaphoreType.DMA((3 * n_ax,)),
        ],
        compiler_params=pltpu.CompilerParams(collective_id=0, has_side_effects=True, vmem_limit_bytes=8 << 20),
    )(*(pltpu.with_memory_space_constraint(x, pltpu.HBM) for x in (velocity, cycle_map)))


def solution(mesh):
    n_ax, n_rad = mesh.shape["ax"], mesh.shape["rad"]
    spec = P(None, "rad", "ax", None)
    body = functools.partial(shards, n_ax, n_rad)
    return jax.shard_map(body, mesh=mesh, in_specs=(spec, P()), out_specs=spec, check_vma=False)
```

profile of v0, /device:TPU:1, one launch (start us, length us, event | category | flops | bytes accessed | tf_op | source)
XLA Modules:
  0.0 17.8 jit_solution(14196215932095643542)
XLA Ops:
  0.0 17.1 %shard_map.28 = f32[3,3,3,768]{3,2,1,0:T(4,128)S(1)} custom-call(f32[3,3,3,768]{3,2,1,0:T(4,128)} %v_hbm.1, s32[3,768]{1,0:T(4,128)} %map_hbm.1), custom_call_target="tpu_custom_call" | custom-call | tf_op jit(solution)/shard_map/pallas_call | solution.py:483
  17.1 0.6 %copy.4 = f32[3,3,3,768]{3,2,1,0:T(4,128)} copy(f32[3,3,3,768]{3,2,1,0:T(4,128)S(1)} %shard_map.28) | data formatting | bytes 165888
where the time goes:
time: 17.9 us; the launch traced here: 17.8 us
  Pallas kernels  17.1 us (96%)
  local copies, waits for them, and re-layouts  0.65 us (4%)
    pallas_call x1, Pallas kernels, shards(): pl.pallas_call(functools.partial(kernel, n_ax, n_rad), out_shape=jax.Shap...  17.1 us
    unnamed x1, local copies, waits for them, and re-layouts  0.65 us

commit v1 on v0

--- a/solution.py
+++ b/solution.py
@@ -16,6 +16,7 @@
 SIGNS = (1.0, -1.0, -1.0)
 EPSILON = 1e-06
 MESH = pl.DeviceIdType.MESH
+IN, SEND, HALO, EDGE, SUMS, SEMS = 0, 2, 5, 9, 11, 14
 
 
 def pair(a, b):
@@ -114,18 +115,19 @@
 
 
 def stages(n_ax):
-    distances, own, beside = [1], 2, 1
-    while own < n_ax // 2:
-        distances.append(own)
-        own, beside = 2 * own, beside + own
-    while beside < n_ax // 2:
-        distances.append(1)
-        beside += 1
+    distances, reach = [], 2
+    while reach < n_ax // 2:
+        distances.append(reach)
+        reach *= 2
     return distances
 
 
+def offsets(n_ax):
+    return sorted({o % n_ax for o in (0, 1, 2, -1, -2)})
+
+
 def kernel(n_ax, n_rad, v_hbm, map_hbm, out_ref, nat, map_ref, own, maps, ext, hx, part, parts, edge_coef,
-           z_out, z_in, z_seg, ready, in_sems, halo_send, halo_recv, h_send, h_recv, p_send, p_recv):
+           z_out, z_in, z_seg, ready, sems):
     rad = lax.axis_index("rad")
     ax = lax.axis_index("ax")
     R, Z, T = nat.shape[1], nat.shape[2], nat.shape[3]
@@ -143,10 +145,16 @@
     def greet(to_ax, to_rad):
         pl.semaphore_signal(barrier, inc=1, device_id=(to_ax, to_rad), device_id_type=MESH)
 
-    greet(left, rad)
-    greet(right, rad)
-    pl.when(has_lo)(lambda: greet(ax, rad - 1))
-    pl.when(has_hi)(lambda: greet(ax, rad + 1))
+    reach = offsets(n_ax)
+
+    def greet_row(to_rad):
+        for o in reach:
+            greet(lax.rem(ax + o, n_ax), to_rad)
+
+    for o in reach[1:]:
+        greet(lax.rem(ax + o, n_ax), rad)
+    pl.when(has_lo)(lambda: greet_row(rad - 1))
+    pl.when(has_hi)(lambda: greet_row(rad + 1))
 
     distances = stages(n_ax)
 
@@ -158,9 +166,9 @@
     def hear(stage):
         pl.semaphore_wait(ready.at[stage], 2)
 
-    fetch = pltpu.make_async_copy(v_hbm, nat, in_sems.at[0])
+    fetch = pltpu.make_async_copy(v_hbm, nat, sems.at[IN])
     fetch.start()
-    fetch_map = pltpu.make_async_copy(map_hbm, map_ref, in_sems.at[1])
+    fetch_map = pltpu.make_async_copy(map_hbm, map_ref, sems.at[IN + 1])
     pl.when(rad == 0)(lambda: fetch_map.start())
     fetch.wait()
     for c in range(3):
@@ -224,57 +232,50 @@
                     row = k * n_rows + (c * R + r) * 2
                     z_out[side, row : row + 2, :] = nat[c, r, first : first + 2, k * LANES : (k + 1) * LANES]
 
-    pl.semaphore_wait(barrier, 2 + jnp.where(has_lo, 1, 0) + jnp.where(has_hi, 1, 0))
+    pl.semaphore_wait(barrier, len(reach) * (1 + jnp.where(has_lo, 1, 0) + jnp.where(has_hi, 1, 0)) - 1)
 
     def z_halo(slot, to_ax):
         return pltpu.make_async_remote_copy(
-            src_ref=z_out.at[slot], dst_ref=z_in.at[slot], send_sem=halo_send.at[slot],
-            recv_sem=halo_recv.at[slot], device_id=(to_ax, rad), device_id_type=MESH)
+            src_ref=z_out.at[slot], dst_ref=z_in.at[slot], send_sem=sems.at[SEND],
+            recv_sem=sems.at[HALO + slot], device_id=(to_ax, rad), device_id_type=MESH)
 
     z_lo, z_hi = z_halo(0, right), z_halo(1, left)
     z_lo.start()
     z_hi.start()
-    tell(0)
+    if distances:
+        tell(0)
 
     rows, cols = pl.ds(1, R), pl.ds(2, Z)
 
-    def halo(slot, src, dst, to_ax, to_rad):
+    def halo(side, src, dst, to_ax, to_rad):
         return pltpu.make_async_remote_copy(
-            src_ref=ext.at[src], dst_ref=ext.at[dst], send_sem=halo_send.at[slot],
-            recv_sem=halo_recv.at[slot], device_id=(to_ax, to_rad), device_id_type=MESH)
+            src_ref=ext.at[src], dst_ref=ext.at[dst], send_sem=sems.at[SEND + 1 + side],
+            recv_sem=sems.at[HALO + 2 + side], device_id=(to_ax, to_rad), device_id_type=MESH)
+
+    def drain(sem, amount):
+        pltpu.make_async_copy(z_seg.at[pl.ds(0, amount)], z_seg.at[pl.ds(0, amount)], sems.at[sem]).wait()
 
     everything = slice(None)
 
     out_going = [
-        halo(2, (everything, R, cols), (everything, 0, cols), ax, rad + 1),
-        halo(3, (everything, R, Z + 1), (everything, 0, 1), right, rad + 1),
-        halo(4, (everything, R, 2), (everything, 0, Z + 2), left, rad + 1),
+        halo(0, (everything, R, cols), (everything, 0, cols), ax, rad + 1),
+        halo(0, (everything, R, Z + 1), (everything, 0, 1), right, rad + 1),
+        halo(0, (everything, R, 2), (everything, 0, Z + 2), left, rad + 1),
     ]
     in_going = [
-        halo(5, (everything, 1, cols), (everything, R + 1, cols), ax, rad - 1),
-        halo(6, (everything, 1, Z + 1), (everything, R + 1, 1), right, rad - 1),
-        halo(7, (everything, 1, 2), (everything, R + 1, Z + 2), left, rad - 1),
+        halo(1, (everything, 1, cols), (everything, R + 1, cols), ax, rad - 1),
+        halo(1, (everything, 1, Z + 1), (everything, R + 1, 1), right, rad - 1),
+        halo(1, (everything, 1, 2), (everything, R + 1, Z + 2), left, rad - 1),
     ]
 
     def start_all(copies):
         for copy in copies:
             copy.start()
 
-    def wait_recv(copies):
-        for copy in copies:
-            copy.wait_recv()
-
-    def wait_send(copies):
-        for copy in copies:
-            copy.wait_send()
-
-    pl.when(has_hi)(lambda: start_all(out_going[:1]))
-    pl.when(has_lo)(lambda: start_all(in_going[:1]))
-    for stage in range(len(distances) - 1)[:1]:
-        hear(stage)
-        tell(stage + 1)
-    pl.when(has_hi)(lambda: start_all(out_going[1:]))
-    pl.when(has_lo)(lambda: start_all(in_going[1:]))
+    rim = 3 * (Z + 2) * SUB
+
+    pl.when(has_hi)(lambda: start_all(out_going))
+    pl.when(has_lo)(lambda: start_all(in_going))
     for side, copy, first in ((0, z_lo, 0), (1, z_hi, Z + 2)):
         copy.wait_recv()
         tiles = [z_in[side, k * n_rows : (k + 1) * n_rows, :] for k in range(T // LANES)]
@@ -285,9 +286,6 @@
                 for z in range(2):
                     row = (side * n_rows + (c * R + r) * 2 + z) * SUB
                     ext[c, r + 1, first + z] = z_seg[row : row + SUB, :]
-    for stage in range(1, len(distances) - 1):
-        hear(stage)
-        tell(stage + 1)
 
     long = [ext[c, 1 : R + 1, 0 : Z + 4] for c in range(3)]
     mids = [x[:, 1:-1] for x in long]
@@ -302,8 +300,8 @@
         product = smooth_t(smooth_z(mids[c] * mids[a]))
         leonards.append(product - w_own[c][:, 1:-1] * w_own[a][:, 1:-1])
 
-    pl.when(has_lo)(lambda: wait_recv(out_going))
-    pl.when(has_hi)(lambda: wait_recv(in_going))
+    pl.when(has_lo)(lambda: drain(HALO + 2, rim))
+    pl.when(has_hi)(lambda: drain(HALO + 3, rim))
 
     @pl.when(rad == 0)
     def _():
@@ -353,16 +351,11 @@
         peer = lax.rem(ax + i, n_ax)
         return pltpu.make_async_remote_copy(
             src_ref=part, dst_ref=parts.at[(1 - side) * n_ax + ax],
-            send_sem=p_send.at[(1 + side) * n_ax + i], recv_sem=p_recv.at[(1 - side) * n_ax + ax],
+            send_sem=sems.at[SEND + (0, 1, 2)[side]], recv_sem=sems.at[SUMS + 1 - side],
             device_id=(peer, rad + side), device_id_type=MESH)
 
-    def sums_in(side, i):
-        peer = lax.rem(ax + i, n_ax)
-        slot = (1 + side) * n_ax + peer
-        return pltpu.make_async_remote_copy(
-            src_ref=part, dst_ref=parts.at[slot],
-            send_sem=p_send.at[(1 + side) * n_ax + i], recv_sem=p_recv.at[slot],
-            device_id=(peer, rad + side), device_id_type=MESH)
+    def sums_in(side, amount):
+        pltpu.make_async_copy(parts.at[pl.ds(0, amount)], parts.at[pl.ds(0, amount)], sems.at[SUMS + 1 + side]).wait()
 
     def first_of(side):
         return 1 if side == 0 else 0
@@ -371,8 +364,11 @@
         first = first_of(side)
         each(n_ax - first, lambda i: sums(side, i + first).start())
 
+    for stage in range(len(distances)):
+        hear(stage)
+        if stage + 1 < len(distances):
+            tell(stage + 1)
     send_sums(0)
-    hear(len(distances) - 1)
     pl.when(has_lo)(lambda: send_sums(-1))
     pl.when(has_hi)(lambda: send_sums(1))
 
@@ -381,8 +377,8 @@
 
     def edge(slot, src, dst, to_rad):
         return pltpu.make_async_remote_copy(
-            src_ref=hx.at[:, src], dst_ref=hx.at[:, dst], send_sem=h_send.at[slot],
-            recv_sem=h_recv.at[slot], device_id=(ax, to_rad), device_id_type=MESH)
+            src_ref=hx.at[:, src], dst_ref=hx.at[:, dst], send_sem=sems.at[SEND + 1 + slot],
+            recv_sem=sems.at[EDGE + slot], device_id=(ax, to_rad), device_id_type=MESH)
 
     edge_out = edge(0, R, 0, rad + 1)
     edge_in = edge(1, 1, R + 1, rad - 1)
@@ -414,7 +410,7 @@
         turns.append(along[:, 2:] - along[:, :-2] + (up(turn) - down(turn)))
 
     count = n_ax * Z * T
-    each(n_ax - 1, lambda i: sums_in(0, i + 1).wait_recv())
+    sums_in(0, n_ax - 1)
 
     def coefficients(total):
         total = jnp.broadcast_to(jnp.sum(jnp.where(group, total, 0.0), axis=1, keepdims=True), (SUB, LANES)) / count
@@ -433,7 +429,7 @@
     coef = coefficients(total_of(0))
 
     def beside(side, row):
-        each(n_ax, lambda i: sums_in(side, i).wait_recv())
+        sums_in(side, n_ax)
         edge_coef[0 if side < 0 else 1] = jnp.broadcast_to(
             coefficients(total_of(side))[row : row + 1], (SUB, LANES))
 
@@ -463,19 +459,10 @@
             for k, tile in enumerate(joined(strips(c, r), wide, pad)):
                 out_ref[c, r, :, k * LANES : (k + 1) * LANES] = tile
 
-    wait_send([z_lo, z_hi])
-
-    @pl.when(has_hi)
-    def _():
-        wait_send(out_going + [edge_out])
-        each(n_ax, lambda i: sums(1, i).wait_send())
-
-    @pl.when(has_lo)
-    def _():
-        wait_send(in_going + [edge_in])
-        each(n_ax, lambda i: sums(-1, i).wait_send())
-
-    each(n_ax - 1, lambda i: sums(0, i + 1).wait_send())
+    drain(SEND, 2 * n_rows * T // LANES + n_ax - 1)
+    beyond = rim + 3 * Z * SUB + n_ax
+    pl.when(has_hi)(lambda: drain(SEND + 1, beyond))
+    pl.when(has_lo)(lambda: drain(SEND + 2, beyond))
 
 
 def shards(n_ax, n_rad, velocity, cycle_map):
@@ -497,15 +484,9 @@
             pltpu.VMEM((2, SUB, LANES), jnp.float32),
             pltpu.VMEM((2, 3 * R * 2 * T // LANES, LANES), jnp.float32),
             pltpu.VMEM((2, 3 * R * 2 * T // LANES, LANES), jnp.float32),
-            pltpu.VMEM((2 * 3 * R * 2 * SUB, LANES), jnp.float32),
-            pltpu.SemaphoreType.REGULAR((len(stages(n_ax)),)),
-            pltpu.SemaphoreType.DMA((2,)),
-            pltpu.SemaphoreType.DMA((8,)),
-            pltpu.SemaphoreType.DMA((8,)),
-            pltpu.SemaphoreType.DMA((2,)),
-            pltpu.SemaphoreType.DMA((2,)),
-            pltpu.SemaphoreType.DMA((3 * n_ax,)),
-            pltpu.SemaphoreType.DMA((3 * n_ax,)),
+            pltpu.VMEM((2 * 3 * R * 2 * SUB + 3 * (Z + 2) * SUB + 2 * n_ax, LANES), jnp.float32),
+            pltpu.SemaphoreType.REGULAR((max(1, len(stages(n_ax))),)),
+            pltpu.SemaphoreType.DMA((SEMS,)),
         ],
         compiler_params=pltpu.CompilerParams(collective_id=0, has_side_effects=True, vmem_limit_bytes=8 << 20),
     )(*(pltpu.with_memory_space_constraint(x, pltpu.HBM) for x in (velocity, cycle_map)))

time: 17.9 us -> 17.3 us (0.966)
  Pallas kernels: 17.1 us -> 16.5 us
    pallas_call x1, Pallas kernels: 17.1 us -> 16.5 us  [shards(): pl.pallas_call(functools.partial(kernel, n_ax, n_rad), out_shape=jax.Shap...]
where the time goes in v1:
time: 17.3 us; the launch traced here: 17.2 us
  Pallas kernels  16.5 us (95%)
  local copies, waits for them, and re-layouts  0.65 us (4%)
    pallas_call x1, Pallas kernels, shards(): pl.pallas_call(functools.partial(kernel, n_ax, n_rad), out_shape=jax.Shap...  16.5 us
    unnamed x1, local copies, waits for them, and re-layouts  0.65 us

profile of v1, /device:TPU:1, one launch (start us, length us, event | category | flops | bytes accessed | tf_op | source)
XLA Modules:
  0.0 17.2 jit_solution(1826171505982349680)
XLA Ops:
  0.0 16.5 %shard_map.28 = f32[3,3,3,768]{3,2,1,0:T(4,128)S(1)} custom-call(f32[3,3,3,768]{3,2,1,0:T(4,128)} %v_hbm.1, s32[3,768]{1,0:T(4,128)} %map_hbm.1), custom_call_target="tpu_custom_call" | custom-call | tf_op jit(solution)/shard_map/pallas_call | solution.py:470
  16.5 0.6 %copy.4 = f32[3,3,3,768]{3,2,1,0:T(4,128)} copy(f32[3,3,3,768]{3,2,1,0:T(4,128)S(1)} %shard_map.28) | data formatting | bytes 165888

commit v2 on v1

v2 whole, which is shorter than its diff:
```python
import functools

import jax
import jax.numpy as jnp
from jax import lax
from jax.experimental import pallas as pl
from jax.experimental.pallas import tpu as pltpu
from jax.sharding import PartitionSpec as P

NRING = 3
MOSTSEG = 16
SUB = 8
LANES = 128
PAIRS = ((0, 0), (1, 1), (2, 2), (0, 1), (0, 2), (1, 2))
SIGNS = (1.0, -1.0, -1.0)
EPSILON = 1e-06
MESH = pl.DeviceIdType.MESH
IN, SEND, ZL, ZR, ROW, LATE, EDGE, SUMS, SEMS = 0, 2, 5, 6, 7, 9, 12, 14, 17


def pair(a, b):
    return PAIRS.index((min(a, b), max(a, b)))


def each(count, body):
    if count <= 16:
        for i in range(count):
            body(i)
    else:
        lax.fori_loop(0, count, lambda i, c: (body(i), c)[1], 0)


def roll(x, shift, axis):
    size = x.shape[axis]
    return pltpu.roll(x, shift % size, axis)


def up(x):
    return roll(x, -1, x.ndim - 1)


def down(x):
    return roll(x, 1, x.ndim - 1)


def smooth_t(x):
    return (down(x) + up(x)) + (x + x)


def smooth_z(x):
    y = x[:-1] + x[1:]
    return y[:-1] + y[1:]


def tiles_of(x):
    return [x[:, k : k + LANES] for k in range(0, x.shape[1], LANES)]


def segments(x, wide, pad):
    rows, tiles = x[0].shape[0], len(x)
    total = tiles * LANES
    lane = lax.broadcasted_iota(jnp.int32, (rows, LANES), 1)
    pieces = []
    for s in range(SUB):
        start = (s * wide - pad) % total
        k, off = start // LANES, start % LANES
        first = x[k]
        if off:
            k2 = (k + 1) % tiles
            second = x[k2]
            first = jnp.where(lane < LANES - off, roll(first, -off, 1), roll(second, -off, 1))
        pieces.append(first)
    return pieces


def joined(pieces, wide, pad):
    rows = pieces[0].shape[0]
    lane = lax.broadcasted_iota(jnp.int32, (rows, LANES), 1)
    tiles = []
    for k in range(SUB * wide // LANES):
        lo, hi = k * LANES, (k + 1) * LANES
        s = lo // wide
        out = None
        while s * wide < hi:
            part = roll(pieces[s], s * wide - pad - lo, 1)
            out = part if out is None else jnp.where(lane >= s * wide - lo, part, out)
            s += 1
        tiles.append(out)
    return tiles


def tensor(grads):
    terms = [grads[c][c] + grads[c][c] if c == a else grads[c][a] + grads[a][c] for c, a in PAIRS]
    squares = [x * x for x in terms]
    total = 0.5 * (squares[0] + squares[1] + squares[2]) + (squares[3] + squares[4] + squares[5])
    return terms, jnp.sqrt(total)


def stages(n_ax):
    distances, reach = [], 2
    while reach < n_ax // 2:
        distances.append(reach)
        reach *= 2
    return distances


def kernel(n_ax, n_rad, v_hbm, map_hbm, out_ref, nat, map_ref, maps, masks, ext, hz, hw, hf, hr, hq, hl, hc, wsc,
           flux, hx, res, acc, part, parts, edge_coef, spare, ready, sems):
    rad = lax.axis_index("rad")
    ax = lax.axis_index("ax")
    R, Z, T = nat.shape[1], nat.shape[2], nat.shape[3]
    K = T // LANES
    wide = T // SUB
    pad = (LANES - wide) // 2
    half = SUB // 2
    near, far = hw.shape[2], 2 - hw.shape[2]
    right, left = lax.rem(ax + 1, n_ax), lax.rem(ax + n_ax - 1, n_ax)
    has_lo, has_hi = rad > 0, rad < n_rad - 1
    first, last, second = ax == 0, ax == n_ax - 1, ax == n_ax - 2

    barrier = pltpu.get_barrier_semaphore()

    def greet(offset, to_rad):
        peer = (lax.rem(ax + offset + n_ax, n_ax), to_rad)
        pl.semaphore_signal(barrier, inc=1, device_id=peer, device_id_type=MESH)

    def greet_row(to_rad, offsets):
        for o in offsets:
            greet(o, to_rad)

    def greet_all(offsets, beside):
        greet_row(rad, offsets)
        pl.when(has_lo)(lambda: greet_row(rad - 1, offsets + beside))
        pl.when(has_hi)(lambda: greet_row(rad + 1, offsets + beside))

    greet_all((-1, -2), (0,))
    pl.when(ax + 1 < n_ax)(lambda: greet_all((1,), ()))
    pl.when(ax + 2 < n_ax)(lambda: greet_all((2,), ()))

    fetch = pltpu.make_async_copy(v_hbm, nat, sems.at[IN])
    fetch.start()
    fetch_map = pltpu.make_async_copy(map_hbm, map_ref, sems.at[IN + 1])
    fetch_map.start()

    distances = stages(n_ax)

    def tell(stage):
        d = distances[stage]
        for peer in (lax.rem(ax + d, n_ax), lax.rem(ax + n_ax - d, n_ax)):
            pl.semaphore_signal(ready.at[stage], inc=1, device_id=(peer, rad), device_id_type=MESH)

    def hear(stage):
        pl.semaphore_wait(ready.at[stage], 2)

    def drain(sem, amount):
        pltpu.make_async_copy(spare.at[pl.ds(0, amount)], spare.at[pl.ds(0, amount)], sems.at[sem]).wait()

    def send(src, dst, group, recv, to_ax, to_rad):
        pltpu.make_async_remote_copy(
            src_ref=src, dst_ref=dst, send_sem=sems.at[SEND + group], recv_sem=sems.at[recv],
            device_id=(to_ax, to_rad), device_id_type=MESH).start()

    beside_sum = jnp.where(has_lo, 1, 0) + jnp.where(has_hi, 1, 0)
    row_sum = 4 - jnp.where(first, 2, 0) - jnp.where(ax == 1, 1, 0)
    pl.semaphore_wait(barrier, row_sum * (1 + beside_sum) + beside_sum)

    send(v_hbm.at[:, :, pl.ds(Z - 2, 2)], hz.at[0], 0, ZL, right, rad)

    @pl.when(last)
    def _():
        send(v_hbm.at[:, :, pl.ds(Z - 2 - near, near)], hw, 0, ZL, right, rad)

    if far:
        @pl.when(second)
        def _():
            send(v_hbm.at[:, :, pl.ds(Z - far, far)], hf, 0, ZL, lax.rem(ax + 2, n_ax), rad)

    @pl.when(ax > 0)
    def _():
        send(v_hbm.at[:, :, pl.ds(0, 2)], hz.at[1], 0, ZR, left, rad)

    def rim(side, group, row, to_rad):
        send(v_hbm.at[:, row, pl.ds(Z - 1, 1)], hr.at[side, :, pl.ds(0, 1)], group, ROW + side, right, to_rad)

        @pl.when(last)
        def _():
            send(v_hbm.at[:, row, pl.ds(Z - 3, 2)], hq.at[side], group, ROW + side, right, to_rad)

        @pl.when(ax > 0)
        def _():
            send(v_hbm.at[:, row, pl.ds(0, 1)], hr.at[side, :, pl.ds(Z + 1, 1)], group, ROW + side, left, to_rad)

        send(v_hbm.at[:, row], hr.at[side, :, pl.ds(1, Z)], group, ROW + side, ax, to_rad)

    pl.when(has_hi)(lambda: rim(0, 1, R - 1, rad + 1))
    pl.when(has_lo)(lambda: rim(1, 2, 0, rad - 1))
    pl.when(ax > 1)(lambda: tell(0))

    def row_of(b, c, r, i):
        return (((b * 3 + c) * (R + 2) + r) * (Z + 4) + i) * SUB

    def get(b, c, r, i, n):
        row = row_of(b, c, r, i)
        return ext[row : row + n * SUB, :].reshape(n, SUB, LANES)

    def put(b, c, r, i, x):
        row = row_of(b, c, r, i)
        ext[row : row + SUB, :] = x

    def unpack(x, b, c, r, i):
        for s, piece in enumerate(segments(tiles_of(x), wide, pad)):
            ext[pl.ds(row_of(b, c, r, i) + s, x.shape[0], stride=SUB), :] = piece

    lane = lax.broadcasted_iota(jnp.int32, (SUB, LANES), 1)
    steps = []
    while 2 ** len(steps) < MOSTSEG:
        steps.append(2 ** len(steps))
    S = len(steps)

    def spread(ring, x):
        total, rest = x, x
        for k, d in enumerate(steps):
            total = total + masks[ring, k] * roll(total, d, x.ndim - 1)
            rest = rest + masks[ring, S + k] * roll(rest, -d, x.ndim - 1)
        return total + rest - x

    def coarsen(ring, b, r, i, count):
        mean = jnp.concatenate([get(b, c, r, i, count) for c in range(3)], axis=0)
        mean = spread(ring, mean) * masks[ring, 2 * S]
        low = roll(roll(mean, -wide, 2), 1, 1)
        high = roll(roll(mean, wide, 2), -1, 1)
        mean = jnp.where(lane < pad, low, mean)
        mean = jnp.where(lane >= pad + wide, high, mean)
        for c in range(3):
            for k in range(count):
                put(b, c, r, i + k, mean[c * count + k])

    def coarsen_block(b, first_i, count):
        @pl.when(rad == 0)
        def _():
            for r in range(NRING):
                coarsen(r, b, r + 1, first_i, count)

    def coarsen_below(b, first_i, count):
        if R == NRING:
            @pl.when(rad == 1)
            def _():
                coarsen(R - 1, b, 0, first_i, count)

    fetch_map.wait()

    @pl.when(rad <= (1 if R == NRING else 0))
    def _():
        labels = map_ref[...].astype(jnp.float32)
        for s, piece in enumerate(segments(tiles_of(labels), wide, pad)):
            maps[pl.ds(s, NRING, stride=SUB), :] = piece
        for ring in range(NRING):
            label = maps[ring * SUB : (ring + 1) * SUB, :]
            for k, d in enumerate(steps):
                masks[ring, k] = (roll(label, d, 1) == label).astype(jnp.float32)
                masks[ring, S + k] = (roll(label, -d, 1) == label).astype(jnp.float32)
            masks[ring, 2 * S] = 1.0 / spread(ring, jnp.ones((SUB, LANES), jnp.float32))

    fetch.wait()
    for c in range(3):
        for r in range(R):
            unpack(nat[c, r], 0, c, r + 1, 2)
    coarsen_block(0, 2, Z)

    @pl.when(ax < 2)
    def _():
        hear(0)
        tell(0)

    @pl.when(first)
    def _():
        send(v_hbm.at[:, :, pl.ds(0, 2)], hl, 0, LATE, left, rad)
        pl.when(has_hi)(lambda: send(v_hbm.at[:, R - 1, pl.ds(0, 1)], hc.at[0], 1, LATE + 1, left, rad + 1))
        pl.when(has_lo)(lambda: send(v_hbm.at[:, 0, pl.ds(0, 1)], hc.at[1], 2, LATE + 2, left, rad - 1))

    def rim_in(side, row):
        line = 3 * K
        pl.when(first)(lambda: drain(ROW + side, line * (Z + 4)))
        pl.when(last)(lambda: drain(ROW + side, line * (Z + 1)))
        pl.when((ax > 0) & (ax < n_ax - 1))(lambda: drain(ROW + side, line * (Z + 2)))
        for c in range(3):
            unpack(hr[side, c], 0, c, row, 1)

        @pl.when(first)
        def _():
            for c in range(3):
                unpack(hq[side, c], 1, c, row, Z - 1)
                unpack(hr[side, c, 0:1], 1, c, row, Z + 1)

    pl.when(has_lo)(lambda: rim_in(0, 0))
    pl.when(has_hi)(lambda: rim_in(1, R + 1))
    coarsen_below(0, 1, Z + 2)
    pl.when(first)(lambda: coarsen_below(1, Z - 1, 3))
    block = 3 * R * K

    @pl.when(first)
    def _():
        drain(ZL, block * 4)
        for c in range(3):
            for r in range(R):
                if far:
                    unpack(hf[c, r], 1, c, r + 1, Z - 2)
                unpack(hw[c, r], 1, c, r + 1, Z - near)
                unpack(hz[0, c, r], 1, c, r + 1, Z)
        coarsen_block(1, Z - 2, 4)
        for c in range(3):
            for r in range(1, R + 1):
                for i in range(2):
                    put(0, c, r, i, get(1, c, r, Z + i, 1)[0])
                    put(1, c, r, Z + 2 + i, get(0, c, r, 2 + i, 1)[0])
            for r in (0, R + 1):
                put(1, c, r, Z + 2, get(0, c, r, 2, 1)[0])

    @pl.when(ax > 0)
    def _():
        drain(ZL, block * 2)
        for c in range(3):
            for r in range(R):
                unpack(hz[0, c, r], 0, c, r + 1, 0)
        coarsen_block(0, 0, 2)

    @pl.when(ax < n_ax - 1)
    def _():
        drain(ZR, block * 2)
        for c in range(3):
            for r in range(R):
                unpack(hz[1, c, r], 0, c, r + 1, Z + 2)
        coarsen_block(0, Z + 2, 2)

    def ends(b, first_i, count):
        @pl.when(rad == 0)
        def _():
            for c in range(3):
                for i in range(first_i, first_i + count):
                    put(b, c, 0, i, SIGNS[c] * roll(get(b, c, 1, i, 1)[0], half, 0))

        @pl.when(rad == n_rad - 1)
        def _():
            for c in range(3):
                for i in range(first_i, first_i + count):
                    put(b, c, R + 1, i, jnp.zeros((SUB, LANES), jnp.float32))

    def phase(b, low_z, high_z):
        n, i0 = high_z - low_z, low_z + 2
        for r in range(1, R + 1):
            grads = []
            for c in range(3):
                long = get(b, c, r, i0 - 2, n + 4)
                after, before = up(long), down(long)
                wsc[c, r, 0 : n + 2] = smooth_z((after + before) + (long + long))
                grads.append([
                    long[2:] - long[:-2],
                    get(b, c, r + 1, i0 - 1, n + 2) - get(b, c, r - 1, i0 - 1, n + 2),
                    after[1:-1] - before[1:-1],
                ])
            terms, size = tensor(grads)
            for p in range(6):
                flux[p, r - 1, 0 : n + 2] = size * terms[p]
        for r in (0, R + 1):
            for c in range(3):
                wsc[c, r, 1 : n + 1] = smooth_t(smooth_z(get(b, c, r, i0 - 1, n + 2)))
        out = []
        for r in range(1, R + 1):
            grads, mids = [], []
            for c in range(3):
                mid = wsc[c, r, 1 : n + 1]
                mids.append(mid)
                grads.append([
                    wsc[c, r, 2 : n + 2] - wsc[c, r, 0:n],
                    wsc[c, r + 1, 1 : n + 1] - wsc[c, r - 1, 1 : n + 1],
                    up(mid) - down(mid),
                ])
            terms, size = tensor(grads)
            size = 0.25 * size
            sums = [[0.0, 0.0], [0.0, 0.0]]
            for p, (c, a) in enumerate(PAIRS):
                product = get(b, c, r, i0 - 1, n + 2) * get(b, a, r, i0 - 1, n + 2)
                leonard = 16.0 * smooth_t(smooth_z(product)) - mids[c] * mids[a]
                model = smooth_t(smooth_z(flux[p, r - 1, 0 : n + 2])) - size * terms[p]
                kind = sums[0 if c == a else 1]
                kind[0] = kind[0] + leonard * model
                kind[1] = kind[1] + model * model
            out.append([sums[0][k] + 2.0 * sums[1][k] for k in range(2)])
        return out

    ends(0, 1, Z + 2)

    @pl.when(first)
    def _():
        ends(1, Z - 1, 4)
        for r, pair_of in enumerate(phase(1, Z - 2, Z)):
            for k in range(2):
                acc[k, r] = jnp.sum(pair_of[k], axis=0)

    @pl.when(ax > 0)
    def _():
        acc[...] = jnp.zeros(acc.shape, jnp.float32)

    sub_index = lax.broadcasted_iota(jnp.int32, (SUB, LANES), 0)
    lane_index = lax.broadcasted_iota(jnp.int32, (SUB, LANES), 1)
    mine = jnp.zeros((SUB, LANES), jnp.float32)
    for r, pair_of in enumerate(phase(0, 0, Z)):
        for k in range(2):
            whole = jnp.sum(pair_of[k][: Z - 2], axis=0)
            rest = jnp.sum(pair_of[k][Z - 2 :], axis=0)
            row = acc[k, r] + whole + jnp.where(last, 0.0, rest)
            row = jnp.sum(row, axis=0, keepdims=True) * (2.0 ** -15, 2.0 ** -14)[k]
            mine = jnp.where(sub_index == k * half + r, row, mine)
    mine = jnp.where((lane_index >= pad) & (lane_index < pad + wide), mine, 0.0)
    fold = LANES // 2
    while fold >= LANES // SUB:
        mine = mine + roll(mine, fold, 1)
        fold //= 2
    group = lane_index // (LANES // SUB) == sub_index
    part[...] = jnp.sum(jnp.where(group, mine, 0.0), axis=0, keepdims=True)

    def sums(side, i):
        peer = lax.rem(ax + i, n_ax)
        send(part, parts.at[(1 - side) * n_ax + ax], (0, 1, 2)[side], SUMS + 1 - side, peer, rad + side)

    def sums_in(side, amount):
        pltpu.make_async_copy(parts.at[pl.ds(0, amount)], parts.at[pl.ds(0, amount)], sems.at[SUMS + 1 + side]).wait()

    def first_of(side):
        return 1 if side == 0 else 0

    def send_sums(side):
        start = first_of(side)
        each(n_ax - start, lambda i: sums(side, i + start))

    pl.when(ax > 1)(lambda: hear(0))
    for stage in range(1, len(distances)):
        tell(stage)
        hear(stage)
    send_sums(0)
    pl.when(has_lo)(lambda: send_sums(-1))
    pl.when(has_hi)(lambda: send_sums(1))

    @pl.when(last)
    def _():
        drain(LATE, block * 2)
        for c in range(3):
            for r in range(R):
                unpack(hl[c, r], 0, c, r + 1, Z + 2)
        coarsen_block(0, Z + 2, 2)

        @pl.when(has_lo)
        def _():
            drain(LATE + 1, 3 * K)
            for c in range(3):
                unpack(hc[0, c], 0, c, 0, Z + 2)

        @pl.when(has_hi)
        def _():
            drain(LATE + 2, 3 * K)
            for c in range(3):
                unpack(hc[1, c], 0, c, R + 1, Z + 2)

        coarsen_below(0, Z + 2, 1)
        ends(0, Z + 2, 1)
        for r in range(1, R + 1):
            grads = []
            for c in range(3):
                long = get(0, c, r, Z, 4)
                mid = long[1:-1]
                grads.append([
                    long[2:] - long[:-2],
                    get(0, c, r + 1, Z + 1, 2) - get(0, c, r - 1, Z + 1, 2),
                    up(mid) - down(mid),
                ])
            terms, size = tensor(grads)
            for p in range(6):
                flux[p, r - 1, Z : Z + 2] = size * terms[p]

    for c in range(3):
        hx[c, 1 : R + 1] = flux[pair(c, 1), :, 1 : Z + 1]
    pl.when(has_hi)(lambda: send(hx.at[:, R], hx.at[:, 0], 1, EDGE, ax, rad + 1))
    pl.when(has_lo)(lambda: send(hx.at[:, 1], hx.at[:, R + 1], 2, EDGE + 1, ax, rad - 1))

    @pl.when(rad == 0)
    def _():
        for c in range(3):
            for z in range(Z):
                hx[c, 0, z] = SIGNS[c] * SIGNS[1] * roll(hx[c, 1, z], half, 0)

    @pl.when(rad == n_rad - 1)
    def _():
        for c in range(3):
            for z in range(Z):
                hx[c, R + 1, z] = jnp.zeros((SUB, LANES), jnp.float32)

    bases, turns = [[], [], []], [[], [], []]
    for r in range(1, R + 1):
        for c in range(3):
            axial = get(0, c, r, 1, Z + 2) * get(0, 0, r, 1, Z + 2)
            outer = get(0, c, r + 1, 2, Z) * get(0, 1, r + 1, 2, Z)
            inner = get(0, c, r - 1, 2, Z) * get(0, 1, r - 1, 2, Z)
            mid = get(0, c, r, 2, Z)
            around = mid * get(0, 2, r, 2, Z)
            change = axial[2:] - axial[:-2] + (outer - inner) + (up(around) - down(around))
            bases[c].append(mid - 0.5 * change)
            turn = flux[pair(c, 2), r - 1, 1 : Z + 1]
            p = pair(c, 0)
            turns[c].append(flux[p, r - 1, 2 : Z + 2] - flux[p, r - 1, 0:Z] + (up(turn) - down(turn)))

    count = n_ax * Z * T
    sums_in(0, n_ax - 1)

    def coefficients(total):
        total = jnp.broadcast_to(jnp.sum(jnp.where(group, total, 0.0), axis=1, keepdims=True), (SUB, LANES)) / count
        return 0.125 * (total / (roll(total, -half, 0) + EPSILON))

    def total_of(side):
        start = first_of(side)
        total = part[...] if start else jnp.zeros((1, LANES), jnp.float32)
        if n_ax <= 16:
            for i in range(start, n_ax):
                total = total + parts[(1 + side) * n_ax + lax.rem(ax + i, n_ax)]
            return total
        return lax.fori_loop(
            start, n_ax, lambda i, t: t + parts[(1 + side) * n_ax + lax.rem(ax + i, n_ax)], total)

    coef = coefficients(total_of(0))

    def beside(side, row):
        sums_in(side, n_ax)
        edge_coef[0 if side < 0 else 1] = jnp.broadcast_to(
            coefficients(total_of(side))[row : row + 1], (SUB, LANES))

    pl.when(has_lo)(lambda: beside(-1, R - 1))
    pl.when(has_hi)(lambda: beside(1, 0))

    @pl.when(rad == 0)
    def _():
        edge_coef[0] = jnp.broadcast_to(coef[0:1], (SUB, LANES))

    @pl.when(rad == n_rad - 1)
    def _():
        edge_coef[1] = jnp.zeros((SUB, LANES), jnp.float32)

    pl.when(has_lo)(lambda: drain(EDGE, 3 * Z * SUB))
    pl.when(has_hi)(lambda: drain(EDGE + 1, 3 * Z * SUB))
    by_row = [edge_coef[0]] + [jnp.broadcast_to(coef[r : r + 1], (SUB, LANES)) for r in range(R)] + [edge_coef[1]]
    for c in range(3):
        for r in range(R):
            new = bases[c][r] + by_row[r + 1] * turns[c][r]
            new = new + (by_row[r + 2] * hx[c, r + 2] - by_row[r] * hx[c, r])
            for z in range(Z):
                row = ((c * R + r) * Z + z) * SUB
                res[row : row + SUB, :] = new[z]
    for c in range(3):
        for r in range(R):
            base = (c * R + r) * Z * SUB
            pieces = [res[pl.ds(base + s, Z, stride=SUB), :] for s in range(SUB)]
            for k, tile in enumerate(joined(pieces, wide, pad)):
                out_ref[c, r, :, k * LANES : (k + 1) * LANES] = tile

    middle = (ax > 0) & (ax < n_ax - 2)

    def sent(group, usual, for_first, for_last, for_second):
        pl.when(middle)(lambda: drain(SEND + group, usual))
        pl.when(first)(lambda: drain(SEND + group, for_first))
        pl.when(last)(lambda: drain(SEND + group, for_last))
        pl.when(second)(lambda: drain(SEND + group, for_second))

    line, total = 3 * K, n_ax - 1
    sent(0, 4 * block + total, 4 * block + total, (4 + near) * block + total, (4 + far) * block + total)
    total = 3 * Z * SUB + n_ax
    usual, more = line * (Z + 2) + total, line * (Z + 4) + total
    pl.when(has_hi)(lambda: sent(1, usual, usual, more, usual))
    pl.when(has_lo)(lambda: sent(2, usual, usual, more, usual))


def shards(n_ax, n_rad, velocity, cycle_map):
    _, R, Z, T = velocity.shape
    near = min(2, Z - 2)
    assert n_ax >= 8 and R >= NRING and Z >= 3

    def vmem(*shape):
        return pltpu.VMEM(shape, jnp.float32)

    return pl.pallas_call(
        functools.partial(kernel, n_ax, n_rad),
        out_shape=jax.ShapeDtypeStruct(velocity.shape, velocity.dtype),
        in_specs=[pl.BlockSpec(memory_space=pltpu.HBM)] * 2,
        out_specs=pl.BlockSpec(memory_space=pltpu.VMEM),
        scratch_shapes=[
            vmem(*velocity.shape),
            pltpu.VMEM(cycle_map.shape, jnp.int32),
            vmem(NRING * SUB, LANES),
            vmem(NRING, 2 * (MOSTSEG - 1).bit_length() + 1, SUB, LANES),
            vmem(2 * 3 * (R + 2) * (Z + 4) * SUB, LANES),
            vmem(2, 3, R, 2, T),
            vmem(3, R, near, T),
            vmem(3, R, max(1, 2 - near), T),
            vmem(2, 3, Z + 2, T),
            vmem(2, 3, 2, T),
            vmem(3, R, 2, T),
            vmem(2, 3, 1, T),
            vmem(3, R + 2, Z + 2, SUB, LANES),
            vmem(6, R, Z + 2, SUB, LANES),
            vmem(3, R + 2, Z, SUB, LANES),
            vmem(3 * R * Z * SUB, LANES),
            vmem(2, R, SUB, LANES),
            vmem(1, LANES),
            vmem(3 * n_ax, 1, LANES),
            vmem(2, SUB, LANES),
            vmem(3 * (R * 6 + Z) * SUB * (T // LANES) + 2 * n_ax, LANES),
            pltpu.SemaphoreType.REGULAR((len(stages(n_ax)),)),
            pltpu.SemaphoreType.DMA((SEMS,)),
        ],
        compiler_params=pltpu.CompilerParams(collective_id=0, has_side_effects=True, vmem_limit_bytes=8 << 20),
    )(*(pltpu.with_memory_space_constraint(x, pltpu.HBM) for x in (velocity, cycle_map)))


def solution(mesh):
    n_ax, n_rad = mesh.shape["ax"], mesh.shape["rad"]
    spec = P(None, "rad", "ax", None)
    body = functools.partial(shards, n_ax, n_rad)
    return jax.shard_map(body, mesh=mesh, in_specs=(spec, P()), out_specs=spec, check_vma=False)
```

time: 17.3 us -> 17.1 us (0.988)
  Pallas kernels: 16.5 us -> 16.3 us
    pallas_call x1, Pallas kernels: 16.5 us -> 16.3 us  [shards(): pl.pallas_call(functools.partial(kernel, n_ax, n_rad), out_shape=jax.Shap...]
where the time goes in v2:
time: 17.1 us; the launch traced here: 16.9 us
  Pallas kernels  16.3 us (95%)
  local copies, waits for them, and re-layouts  0.65 us (4%)
    pallas_call x1, Pallas kernels, shards(): pl.pallas_call(functools.partial(kernel, n_ax, n_rad), out_shape=jax.Shap...  16.3 us
    unnamed x1, local copies, waits for them, and re-layouts  0.65 us

profile of v2, /device:TPU:1, one launch (start us, length us, event | category | flops | bytes accessed | tf_op | source)
XLA Modules:
  0.0 16.9 jit_solution(3341475522353337527)
XLA Ops:
  0.0 16.3 %shard_map.28 = f32[3,3,3,768]{3,2,1,0:T(4,128)S(1)} custom-call(f32[3,3,3,768]{3,2,1,0:T(4,128)} %v_hbm.1, s32[3,768]{1,0:T(4,128)} %map_hbm.1), custom_call_target="tpu_custom_call" | custom-call | tf_op jit(solution)/shard_map/pallas_call | solution.py:587
  16.3 0.6 %copy.4 = f32[3,3,3,768]{3,2,1,0:T(4,128)} copy(f32[3,3,3,768]{3,2,1,0:T(4,128)S(1)} %shard_map.28) | data formatting | bytes 165888

commit v3 on v2

--- a/solution.py
+++ b/solution.py
@@ -104,8 +104,8 @@
     return distances
 
 
-def kernel(n_ax, n_rad, v_hbm, map_hbm, out_ref, nat, map_ref, maps, masks, ext, hz, hw, hf, hr, hq, hl, hc, wsc,
-           flux, hx, res, acc, part, parts, edge_coef, spare, ready, sems):
+def kernel(n_ax, n_rad, v_hbm, map_hbm, out_ref, nat, map_ref, maps, masks, ext, rims, hz, he, hr, hq, hl, hc, wsc,
+           lsc, flux, hx, res, acc, part, parts, edge_coef, spare, ready, sems):
     rad = lax.axis_index("rad")
     ax = lax.axis_index("ax")
     R, Z, T = nat.shape[1], nat.shape[2], nat.shape[3]
@@ -113,7 +113,8 @@
     wide = T // SUB
     pad = (LANES - wide) // 2
     half = SUB // 2
-    near, far = hw.shape[2], 2 - hw.shape[2]
+    near = min(2, Z - 2)
+    far = 2 - near
     right, left = lax.rem(ax + 1, n_ax), lax.rem(ax + n_ax - 1, n_ax)
     has_lo, has_hi = rad > 0, rad < n_rad - 1
     first, last, second = ax == 0, ax == n_ax - 1, ax == n_ax - 2
@@ -164,20 +165,18 @@
     row_sum = 4 - jnp.where(first, 2, 0) - jnp.where(ax == 1, 1, 0)
     pl.semaphore_wait(barrier, row_sum * (1 + beside_sum) + beside_sum)
 
-    send(v_hbm.at[:, :, pl.ds(Z - 2, 2)], hz.at[0], 0, ZL, right, rad)
+    def planes(first_z, count, dst, row, group, recv, to_ax):
+        for r in range(R):
+            send(v_hbm.at[:, r, pl.ds(first_z, count)], dst.at[:, pl.ds(2 * r + row, count)], group, recv, to_ax, rad)
 
     @pl.when(last)
     def _():
-        send(v_hbm.at[:, :, pl.ds(Z - 2 - near, near)], hw, 0, ZL, right, rad)
-
+        planes(Z - 2 - near, near, he, far, 0, ZL, right)
+
+    planes(Z - 2, 2, hz.at[0], 0, 0, ZL, right)
     if far:
-        @pl.when(second)
-        def _():
-            send(v_hbm.at[:, :, pl.ds(Z - far, far)], hf, 0, ZL, lax.rem(ax + 2, n_ax), rad)
-
-    @pl.when(ax > 0)
-    def _():
-        send(v_hbm.at[:, :, pl.ds(0, 2)], hz.at[1], 0, ZR, left, rad)
+        pl.when(second)(lambda: planes(Z - far, far, he, 0, 0, ZL, lax.rem(ax + 2, n_ax)))
+    pl.when(ax > 0)(lambda: planes(0, 2, hz.at[1], 0, 0, ZR, left))
 
     def rim(side, group, row, to_rad):
         send(v_hbm.at[:, row, pl.ds(Z - 1, 1)], hr.at[side, :, pl.ds(0, 1)], group, ROW + side, right, to_rad)
@@ -197,19 +196,36 @@
     pl.when(ax > 1)(lambda: tell(0))
 
     def row_of(b, c, r, i):
-        return (((b * 3 + c) * (R + 2) + r) * (Z + 4) + i) * SUB
+        line, pairs = c * R + r - 1, 3 * R * 2
+        if b:
+            k = i - Z + 2
+            return (3 * R * Z + pairs * (2 + k // 2) + line * 2 + k % 2) * SUB
+        if 2 <= i < Z + 2:
+            return (line * Z + i - 2) * SUB
+        return (3 * R * Z + (line * 2 + i if i < 2 else pairs + line * 2 + i - Z - 2)) * SUB
+
+    def rim_of(b, c, r, i):
+        return (((b * 3 + c) * 2 + (0 if r == 0 else 1)) * (Z + 4) + i) * SUB
+
+    def place(b, c, r, i):
+        inside = 0 < r <= R
+        return (ext, row_of(b, c, r, i)) if inside else (rims, rim_of(b, c, r, i))
 
     def get(b, c, r, i, n):
-        row = row_of(b, c, r, i)
-        return ext[row : row + n * SUB, :].reshape(n, SUB, LANES)
+        blocks = []
+        for k in range(n):
+            ref, row = place(b, c, r, i + k)
+            blocks.append(ref[row : row + SUB, :])
+        return jnp.stack(blocks)
 
     def put(b, c, r, i, x):
-        row = row_of(b, c, r, i)
-        ext[row : row + SUB, :] = x
-
-    def unpack(x, b, c, r, i):
+        ref, row = place(b, c, r, i)
+        ref[row : row + SUB, :] = x
+
+    def unpack(x, target):
+        ref, row = target
         for s, piece in enumerate(segments(tiles_of(x), wide, pad)):
-            ext[pl.ds(row_of(b, c, r, i) + s, x.shape[0], stride=SUB), :] = piece
+            ref[pl.ds(row + s, x.shape[0], stride=SUB), :] = piece
 
     lane = lax.broadcasted_iota(jnp.int32, (SUB, LANES), 1)
     steps = []
@@ -264,7 +280,7 @@
     fetch.wait()
     for c in range(3):
         for r in range(R):
-            unpack(nat[c, r], 0, c, r + 1, 2)
+            unpack(nat[c, r], place(0, c, r + 1, 2))
     coarsen_block(0, 2, Z)
 
     @pl.when(ax < 2)
@@ -274,9 +290,53 @@
 
     @pl.when(first)
     def _():
-        send(v_hbm.at[:, :, pl.ds(0, 2)], hl, 0, LATE, left, rad)
+        planes(0, 2, hl, 0, 0, LATE, left)
         pl.when(has_hi)(lambda: send(v_hbm.at[:, R - 1, pl.ds(0, 1)], hc.at[0], 1, LATE + 1, left, rad + 1))
         pl.when(has_lo)(lambda: send(v_hbm.at[:, 0, pl.ds(0, 1)], hc.at[1], 2, LATE + 2, left, rad - 1))
+
+    def local(b, low_z, high_z):
+        n, i0 = high_z - low_z, low_z + 2
+        for r in range(1, R + 1):
+            longs, filtered = [], []
+            for c in range(3):
+                longs.append(get(b, c, r, i0 - 1, n + 2))
+                filtered.append(smooth_t(smooth_z(get(b, c, r, i0 - 2, n + 4))))
+                wsc[b, c, r, 0 : n + 2] = filtered[c]
+            for p, (c, a) in enumerate(PAIRS):
+                product = smooth_t(smooth_z(longs[c] * longs[a]))
+                lsc[b, p, r - 1, 0:n] = 16.0 * product - filtered[c][1:-1] * filtered[a][1:-1]
+
+    block = 3 * R * K
+
+    @pl.when(first)
+    def _():
+        drain(ZL, block * 4)
+        for c in range(3):
+            unpack(he[c], place(1, c, 1, Z - 2))
+            unpack(hz[0, c], place(1, c, 1, Z))
+        coarsen_block(1, Z - 2, 4)
+        for c in range(3):
+            for r in range(1, R + 1):
+                for i in range(2):
+                    put(0, c, r, i, get(1, c, r, Z + i, 1)[0])
+                    put(1, c, r, Z + 2 + i, get(0, c, r, 2 + i, 1)[0])
+        local(1, Z - 2, Z)
+
+    @pl.when(ax > 0)
+    def _():
+        drain(ZL, block * 2)
+        for c in range(3):
+            unpack(hz[0, c], place(0, c, 1, 0))
+        coarsen_block(0, 0, 2)
+
+    @pl.when(ax < n_ax - 1)
+    def _():
+        drain(ZR, block * 2)
+        for c in range(3):
+            unpack(hz[1, c], place(0, c, 1, Z + 2))
+        coarsen_block(0, Z + 2, 2)
+
+    local(0, 0, Z)
 
     def rim_in(side, row):
         line = 3 * K
@@ -284,53 +344,18 @@
         pl.when(last)(lambda: drain(ROW + side, line * (Z + 1)))
         pl.when((ax > 0) & (ax < n_ax - 1))(lambda: drain(ROW + side, line * (Z + 2)))
         for c in range(3):
-            unpack(hr[side, c], 0, c, row, 1)
+            unpack(hr[side, c], place(0, c, row, 1))
 
         @pl.when(first)
         def _():
             for c in range(3):
-                unpack(hq[side, c], 1, c, row, Z - 1)
-                unpack(hr[side, c, 0:1], 1, c, row, Z + 1)
+                unpack(hq[side, c], place(1, c, row, Z - 1))
+                unpack(hr[side, c, 0:2], place(1, c, row, Z + 1))
 
     pl.when(has_lo)(lambda: rim_in(0, 0))
     pl.when(has_hi)(lambda: rim_in(1, R + 1))
     coarsen_below(0, 1, Z + 2)
-    pl.when(first)(lambda: coarsen_below(1, Z - 1, 3))
-    block = 3 * R * K
-
-    @pl.when(first)
-    def _():
-        drain(ZL, block * 4)
-        for c in range(3):
-            for r in range(R):
-                if far:
-                    unpack(hf[c, r], 1, c, r + 1, Z - 2)
-                unpack(hw[c, r], 1, c, r + 1, Z - near)
-                unpack(hz[0, c, r], 1, c, r + 1, Z)
-        coarsen_block(1, Z - 2, 4)
-        for c in range(3):
-            for r in range(1, R + 1):
-                for i in range(2):
-                    put(0, c, r, i, get(1, c, r, Z + i, 1)[0])
-                    put(1, c, r, Z + 2 + i, get(0, c, r, 2 + i, 1)[0])
-            for r in (0, R + 1):
-                put(1, c, r, Z + 2, get(0, c, r, 2, 1)[0])
-
-    @pl.when(ax > 0)
-    def _():
-        drain(ZL, block * 2)
-        for c in range(3):
-            for r in range(R):
-                unpack(hz[0, c, r], 0, c, r + 1, 0)
-        coarsen_block(0, 0, 2)
-
-    @pl.when(ax < n_ax - 1)
-    def _():
-        drain(ZR, block * 2)
-        for c in range(3):
-            for r in range(R):
-                unpack(hz[1, c, r], 0, c, r + 1, Z + 2)
-        coarsen_block(0, Z + 2, 2)
+    pl.when(first)(lambda: coarsen_below(1, Z - 1, 4))
 
     def ends(b, first_i, count):
         @pl.when(rad == 0)
@@ -351,39 +376,35 @@
             grads = []
             for c in range(3):
                 long = get(b, c, r, i0 - 2, n + 4)
-                after, before = up(long), down(long)
-                wsc[c, r, 0 : n + 2] = smooth_z((after + before) + (long + long))
+                mid = long[1:-1]
                 grads.append([
                     long[2:] - long[:-2],
                     get(b, c, r + 1, i0 - 1, n + 2) - get(b, c, r - 1, i0 - 1, n + 2),
-                    after[1:-1] - before[1:-1],
+                    up(mid) - down(mid),
                 ])
             terms, size = tensor(grads)
             for p in range(6):
                 flux[p, r - 1, 0 : n + 2] = size * terms[p]
         for r in (0, R + 1):
             for c in range(3):
-                wsc[c, r, 1 : n + 1] = smooth_t(smooth_z(get(b, c, r, i0 - 1, n + 2)))
+                wsc[b, c, r, 1 : n + 1] = smooth_t(smooth_z(get(b, c, r, i0 - 1, n + 2)))
         out = []
         for r in range(1, R + 1):
-            grads, mids = [], []
-            for c in range(3):
-                mid = wsc[c, r, 1 : n + 1]
-                mids.append(mid)
+            grads = []
+            for c in range(3):
+                mid = wsc[b, c, r, 1 : n + 1]
                 grads.append([
-                    wsc[c, r, 2 : n + 2] - wsc[c, r, 0:n],
-                    wsc[c, r + 1, 1 : n + 1] - wsc[c, r - 1, 1 : n + 1],
+                    wsc[b, c, r, 2 : n + 2] - wsc[b, c, r, 0:n],
+                    wsc[b, c, r + 1, 1 : n + 1] - wsc[b, c, r - 1, 1 : n + 1],
                     up(mid) - down(mid),
                 ])
             terms, size = tensor(grads)
             size = 0.25 * size
             sums = [[0.0, 0.0], [0.0, 0.0]]
             for p, (c, a) in enumerate(PAIRS):
-                product = get(b, c, r, i0 - 1, n + 2) * get(b, a, r, i0 - 1, n + 2)
-                leonard = 16.0 * smooth_t(smooth_z(product)) - mids[c] * mids[a]
                 model = smooth_t(smooth_z(flux[p, r - 1, 0 : n + 2])) - size * terms[p]
                 kind = sums[0 if c == a else 1]
-                kind[0] = kind[0] + leonard * model
+                kind[0] = kind[0] + lsc[b, p, r - 1, 0:n] * model
                 kind[1] = kind[1] + model * model
             out.append([sums[0][k] + 2.0 * sums[1][k] for k in range(2)])
         return out
@@ -445,21 +466,20 @@
     def _():
         drain(LATE, block * 2)
         for c in range(3):
-            for r in range(R):
-                unpack(hl[c, r], 0, c, r + 1, Z + 2)
+            unpack(hl[c], place(0, c, 1, Z + 2))
         coarsen_block(0, Z + 2, 2)
 
         @pl.when(has_lo)
         def _():
             drain(LATE + 1, 3 * K)
             for c in range(3):
-                unpack(hc[0, c], 0, c, 0, Z + 2)
+                unpack(hc[0, c], place(0, c, 0, Z + 2))
 
         @pl.when(has_hi)
         def _():
             drain(LATE + 2, 3 * K)
             for c in range(3):
-                unpack(hc[1, c], 0, c, R + 1, Z + 2)
+                unpack(hc[1, c], place(0, c, R + 1, Z + 2))
 
         coarsen_below(0, Z + 2, 1)
         ends(0, Z + 2, 1)
@@ -578,7 +598,6 @@
 
 def shards(n_ax, n_rad, velocity, cycle_map):
     _, R, Z, T = velocity.shape
-    near = min(2, Z - 2)
     assert n_ax >= 8 and R >= NRING and Z >= 3
 
     def vmem(*shape):
@@ -594,15 +613,16 @@
             pltpu.VMEM(cycle_map.shape, jnp.int32),
             vmem(NRING * SUB, LANES),
             vmem(NRING, 2 * (MOSTSEG - 1).bit_length() + 1, SUB, LANES),
-            vmem(2 * 3 * (R + 2) * (Z + 4) * SUB, LANES),
-            vmem(2, 3, R, 2, T),
-            vmem(3, R, near, T),
-            vmem(3, R, max(1, 2 - near), T),
+            vmem(3 * R * (Z + 10) * SUB, LANES),
+            vmem(2 * 3 * 2 * (Z + 4) * SUB, LANES),
+            vmem(2, 3, 2 * R, T),
+            vmem(3, 2 * R, T),
             vmem(2, 3, Z + 2, T),
             vmem(2, 3, 2, T),
-            vmem(3, R, 2, T),
+            vmem(3, 2 * R, T),
             vmem(2, 3, 1, T),
-            vmem(3, R + 2, Z + 2, SUB, LANES),
+            vmem(2, 3, R + 2, Z + 2, SUB, LANES),
+            vmem(2, 6, R, Z, SUB, LANES),
             vmem(6, R, Z + 2, SUB, LANES),
             vmem(3, R + 2, Z, SUB, LANES),
             vmem(3 * R * Z * SUB, LANES),

time: 17.1 us -> 16 us (0.936)
  Pallas kernels: 16.3 us -> 15.2 us
    pallas_call x1, Pallas kernels: 16.3 us -> 15.2 us  [shards(): pl.pallas_call(functools.partial(kernel, n_ax, n_rad), out_shape=jax.Shap...]
where the time goes in v3:
time: 16 us; the launch traced here: 15.9 us
  Pallas kernels  15.2 us (95%)
  local copies, waits for them, and re-layouts  0.65 us (4%)
    pallas_call x1, Pallas kernels, shards(): pl.pallas_call(functools.partial(kernel, n_ax, n_rad), out_shape=jax.Shap...  15.2 us
    unnamed x1, local copies, waits for them, and re-layouts  0.65 us

profile of v3, /device:TPU:1, one launch (start us, length us, event | category | flops | bytes accessed | tf_op | source)
XLA Modules:
  0.0 15.9 jit_solution(13538693319860238245)
XLA Ops:
  0.0 15.2 %shard_map.28 = f32[3,3,3,768]{3,2,1,0:T(4,128)S(1)} custom-call(f32[3,3,3,768]{3,2,1,0:T(4,128)} %v_hbm.1, s32[3,768]{1,0:T(4,128)} %map_hbm.1), custom_call_target="tpu_custom_call" | custom-call | tf_op jit(solution)/shard_map/pallas_call | solution.py:606
  15.2 0.6 %copy.4 = f32[3,3,3,768]{3,2,1,0:T(4,128)} copy(f32[3,3,3,768]{3,2,1,0:T(4,128)S(1)} %shard_map.28) | data formatting | bytes 165888

commit v4 on v3

--- a/solution.py
+++ b/solution.py
@@ -104,8 +104,8 @@
     return distances
 
 
-def kernel(n_ax, n_rad, v_hbm, map_hbm, out_ref, nat, map_ref, maps, masks, ext, rims, hz, he, hr, hq, hl, hc, wsc,
-           lsc, flux, hx, res, acc, part, parts, edge_coef, spare, ready, sems):
+def kernel(n_ax, n_rad, v_hbm, map_hbm, out_ref, nat, map_ref, maps, masks, ext, rims, hz, he, hr, hl, hc, wsc,
+           lsc, around, slope, paired, flux, hx, res, acc, part, parts, edge_coef, spare, ready, sems):
     rad = lax.axis_index("rad")
     ax = lax.axis_index("ax")
     R, Z, T = nat.shape[1], nat.shape[2], nat.shape[3]
@@ -169,27 +169,24 @@
         for r in range(R):
             send(v_hbm.at[:, r, pl.ds(first_z, count)], dst.at[:, pl.ds(2 * r + row, count)], group, recv, to_ax, rad)
 
-    @pl.when(last)
-    def _():
-        planes(Z - 2 - near, near, he, far, 0, ZL, right)
-
+    pl.when(last)(lambda: planes(Z - 2 - near, near, he, far, 0, ZL, right))
     planes(Z - 2, 2, hz.at[0], 0, 0, ZL, right)
     if far:
         pl.when(second)(lambda: planes(Z - far, far, he, 0, 0, ZL, lax.rem(ax + 2, n_ax)))
     pl.when(ax > 0)(lambda: planes(0, 2, hz.at[1], 0, 0, ZR, left))
 
     def rim(side, group, row, to_rad):
-        send(v_hbm.at[:, row, pl.ds(Z - 1, 1)], hr.at[side, :, pl.ds(0, 1)], group, ROW + side, right, to_rad)
+        send(v_hbm.at[:, row, pl.ds(Z - 1, 1)], hr.at[side, :, pl.ds(2, 1)], group, ROW + side, right, to_rad)
 
         @pl.when(last)
         def _():
-            send(v_hbm.at[:, row, pl.ds(Z - 3, 2)], hq.at[side], group, ROW + side, right, to_rad)
+            send(v_hbm.at[:, row, pl.ds(Z - 3, 2)], hr.at[side, :, pl.ds(0, 2)], group, ROW + side, right, to_rad)
 
         @pl.when(ax > 0)
         def _():
-            send(v_hbm.at[:, row, pl.ds(0, 1)], hr.at[side, :, pl.ds(Z + 1, 1)], group, ROW + side, left, to_rad)
-
-        send(v_hbm.at[:, row], hr.at[side, :, pl.ds(1, Z)], group, ROW + side, ax, to_rad)
+            send(v_hbm.at[:, row, pl.ds(0, 1)], hr.at[side, :, pl.ds(Z + 3, 1)], group, ROW + side, left, to_rad)
+
+        send(v_hbm.at[:, row], hr.at[side, :, pl.ds(3, Z)], group, ROW + side, ax, to_rad)
 
     pl.when(has_hi)(lambda: rim(0, 1, R - 1, rad + 1))
     pl.when(has_lo)(lambda: rim(1, 2, 0, rad - 1))
@@ -205,7 +202,7 @@
         return (3 * R * Z + (line * 2 + i if i < 2 else pairs + line * 2 + i - Z - 2)) * SUB
 
     def rim_of(b, c, r, i):
-        return (((b * 3 + c) * 2 + (0 if r == 0 else 1)) * (Z + 4) + i) * SUB
+        return ((c * 2 + (0 if r == 0 else 1)) * (Z + 4) + i + 1 - b * Z) * SUB
 
     def place(b, c, r, i):
         inside = 0 < r <= R
@@ -240,28 +237,35 @@
             rest = rest + masks[ring, S + k] * roll(rest, -d, x.ndim - 1)
         return total + rest - x
 
-    def coarsen(ring, b, r, i, count):
-        mean = jnp.concatenate([get(b, c, r, i, count) for c in range(3)], axis=0)
-        mean = spread(ring, mean) * masks[ring, 2 * S]
-        low = roll(roll(mean, -wide, 2), 1, 1)
-        high = roll(roll(mean, wide, 2), -1, 1)
-        mean = jnp.where(lane < pad, low, mean)
-        mean = jnp.where(lane >= pad + wide, high, mean)
-        for c in range(3):
-            for k in range(count):
-                put(b, c, r, i + k, mean[c * count + k])
+    def coarsen(places, count):
+        values = [jnp.concatenate([get(b, c, r, i, count) for c in range(3)], axis=0) for _, b, r, i in places]
+        total, rest = list(values), list(values)
+        for k, d in enumerate(steps):
+            for j, (ring, _, _, _) in enumerate(places):
+                total[j] = total[j] + masks[ring, k] * roll(total[j], d, 2)
+            for j, (ring, _, _, _) in enumerate(places):
+                rest[j] = rest[j] + masks[ring, S + k] * roll(rest[j], -d, 2)
+        means = [(t + q - x) * masks[p[0], 2 * S] for t, q, x, p in zip(total, rest, values, places)]
+        lows = [roll(m, -wide, 2) for m in means]
+        highs = [roll(m, wide, 2) for m in means]
+        lows, highs = [roll(m, 1, 1) for m in lows], [roll(m, -1, 1) for m in highs]
+        for mean, low, high, (_, b, r, i) in zip(means, lows, highs, places):
+            mean = jnp.where(lane < pad, low, mean)
+            mean = jnp.where(lane >= pad + wide, high, mean)
+            for c in range(3):
+                for k in range(count):
+                    put(b, c, r, i + k, mean[c * count + k])
 
     def coarsen_block(b, first_i, count):
         @pl.when(rad == 0)
         def _():
-            for r in range(NRING):
-                coarsen(r, b, r + 1, first_i, count)
-
-    def coarsen_below(b, first_i, count):
+            coarsen([(r, b, r + 1, first_i) for r in range(NRING)], count)
+
+    def coarsen_below(first_i, count):
         if R == NRING:
             @pl.when(rad == 1)
             def _():
-                coarsen(R - 1, b, 0, first_i, count)
+                coarsen([(R - 1, 0, 0, first_i)], count)
 
     fetch_map.wait()
 
@@ -283,6 +287,33 @@
             unpack(nat[c, r], place(0, c, r + 1, 2))
     coarsen_block(0, 2, Z)
 
+    def turns_of(b, i, count):
+        z = i + 2 - b * Z
+        for r in range(1, R + 1):
+            for c in range(3):
+                x = get(b, c, r, i, count)
+                after, before = up(x), down(x)
+                around[c, r - 1, z : z + count] = (after + before) + (x + x)
+                slope[c, r - 1, z : z + count] = after - before
+
+    def products_of(b, i, count):
+        z = i + 2 - b * Z
+        for r in range(1, R + 1):
+            x = [get(b, c, r, i, count) for c in range(3)]
+            for p, (c, a) in enumerate(PAIRS):
+                paired[p, r - 1, z : z + count] = smooth_t(x[c] * x[a])
+
+    def local(b, low_z):
+        n, z = Z - low_z, low_z + 4 - b * Z
+        for r in range(1, R + 1):
+            filtered = []
+            for c in range(3):
+                filtered.append(smooth_z(around[c, r - 1, z - 2 : z + n + 2]))
+                wsc[b, c, r, 0 : n + 2] = filtered[c]
+            for p, (c, a) in enumerate(PAIRS):
+                product = smooth_z(paired[p, r - 1, z - 1 : z + n + 1])
+                lsc[b, p, r - 1, 0:n] = 16.0 * product - filtered[c][1:-1] * filtered[a][1:-1]
+
     @pl.when(ax < 2)
     def _():
         hear(0)
@@ -294,102 +325,40 @@
         pl.when(has_hi)(lambda: send(v_hbm.at[:, R - 1, pl.ds(0, 1)], hc.at[0], 1, LATE + 1, left, rad + 1))
         pl.when(has_lo)(lambda: send(v_hbm.at[:, 0, pl.ds(0, 1)], hc.at[1], 2, LATE + 2, left, rad - 1))
 
-    def local(b, low_z, high_z):
+    def axis_end(b, first_i, count):
+        for c in range(3):
+            for i in range(first_i, first_i + count):
+                put(b, c, 0, i, SIGNS[c] * roll(get(b, c, 1, i, 1)[0], half, 0))
+
+    def wall_end():
+        for c in range(3):
+            for i in range(-1, Z + 3):
+                put(0, c, R + 1, i, jnp.zeros((SUB, LANES), jnp.float32))
+
+    def strain(b, low_z, high_z, rows):
         n, i0 = high_z - low_z, low_z + 2
-        for r in range(1, R + 1):
-            longs, filtered = [], []
-            for c in range(3):
-                longs.append(get(b, c, r, i0 - 1, n + 2))
-                filtered.append(smooth_t(smooth_z(get(b, c, r, i0 - 2, n + 4))))
-                wsc[b, c, r, 0 : n + 2] = filtered[c]
-            for p, (c, a) in enumerate(PAIRS):
-                product = smooth_t(smooth_z(longs[c] * longs[a]))
-                lsc[b, p, r - 1, 0:n] = 16.0 * product - filtered[c][1:-1] * filtered[a][1:-1]
-
-    block = 3 * R * K
-
-    @pl.when(first)
-    def _():
-        drain(ZL, block * 4)
-        for c in range(3):
-            unpack(he[c], place(1, c, 1, Z - 2))
-            unpack(hz[0, c], place(1, c, 1, Z))
-        coarsen_block(1, Z - 2, 4)
-        for c in range(3):
-            for r in range(1, R + 1):
-                for i in range(2):
-                    put(0, c, r, i, get(1, c, r, Z + i, 1)[0])
-                    put(1, c, r, Z + 2 + i, get(0, c, r, 2 + i, 1)[0])
-        local(1, Z - 2, Z)
-
-    @pl.when(ax > 0)
-    def _():
-        drain(ZL, block * 2)
-        for c in range(3):
-            unpack(hz[0, c], place(0, c, 1, 0))
-        coarsen_block(0, 0, 2)
-
-    @pl.when(ax < n_ax - 1)
-    def _():
-        drain(ZR, block * 2)
-        for c in range(3):
-            unpack(hz[1, c], place(0, c, 1, Z + 2))
-        coarsen_block(0, Z + 2, 2)
-
-    local(0, 0, Z)
-
-    def rim_in(side, row):
-        line = 3 * K
-        pl.when(first)(lambda: drain(ROW + side, line * (Z + 4)))
-        pl.when(last)(lambda: drain(ROW + side, line * (Z + 1)))
-        pl.when((ax > 0) & (ax < n_ax - 1))(lambda: drain(ROW + side, line * (Z + 2)))
-        for c in range(3):
-            unpack(hr[side, c], place(0, c, row, 1))
-
-        @pl.when(first)
-        def _():
-            for c in range(3):
-                unpack(hq[side, c], place(1, c, row, Z - 1))
-                unpack(hr[side, c, 0:2], place(1, c, row, Z + 1))
-
-    pl.when(has_lo)(lambda: rim_in(0, 0))
-    pl.when(has_hi)(lambda: rim_in(1, R + 1))
-    coarsen_below(0, 1, Z + 2)
-    pl.when(first)(lambda: coarsen_below(1, Z - 1, 4))
-
-    def ends(b, first_i, count):
-        @pl.when(rad == 0)
-        def _():
-            for c in range(3):
-                for i in range(first_i, first_i + count):
-                    put(b, c, 0, i, SIGNS[c] * roll(get(b, c, 1, i, 1)[0], half, 0))
-
-        @pl.when(rad == n_rad - 1)
-        def _():
-            for c in range(3):
-                for i in range(first_i, first_i + count):
-                    put(b, c, R + 1, i, jnp.zeros((SUB, LANES), jnp.float32))
-
-    def phase(b, low_z, high_z):
-        n, i0 = high_z - low_z, low_z + 2
-        for r in range(1, R + 1):
+        z = low_z + 4 - b * Z
+        for r in rows:
             grads = []
             for c in range(3):
                 long = get(b, c, r, i0 - 2, n + 4)
-                mid = long[1:-1]
                 grads.append([
                     long[2:] - long[:-2],
                     get(b, c, r + 1, i0 - 1, n + 2) - get(b, c, r - 1, i0 - 1, n + 2),
-                    up(mid) - down(mid),
+                    slope[c, r - 1, z - 1 : z + n + 1],
                 ])
             terms, size = tensor(grads)
             for p in range(6):
-                flux[p, r - 1, 0 : n + 2] = size * terms[p]
-        for r in (0, R + 1):
-            for c in range(3):
-                wsc[b, c, r, 1 : n + 1] = smooth_t(smooth_z(get(b, c, r, i0 - 1, n + 2)))
-        out = []
-        for r in range(1, R + 1):
+                flux[b, p, r - 1, 0 : n + 2] = size * terms[p]
+
+    def outside(b, low_z, r):
+        n, i0 = Z - low_z, low_z + 2
+        for c in range(3):
+            wsc[b, c, r, 1 : n + 1] = smooth_t(smooth_z(get(b, c, r, i0 - 1, n + 2)))
+
+    def collect(b, low_z, high_z, rows):
+        n = high_z - low_z
+        for r in rows:
             grads = []
             for c in range(3):
                 mid = wsc[b, c, r, 1 : n + 1]
@@ -402,35 +371,117 @@
             size = 0.25 * size
             sums = [[0.0, 0.0], [0.0, 0.0]]
             for p, (c, a) in enumerate(PAIRS):
-                model = smooth_t(smooth_z(flux[p, r - 1, 0 : n + 2])) - size * terms[p]
+                model = smooth_t(smooth_z(flux[b, p, r - 1, 0 : n + 2])) - size * terms[p]
                 kind = sums[0 if c == a else 1]
                 kind[0] = kind[0] + lsc[b, p, r - 1, 0:n] * model
                 kind[1] = kind[1] + model * model
-            out.append([sums[0][k] + 2.0 * sums[1][k] for k in range(2)])
-        return out
-
-    ends(0, 1, Z + 2)
+            for k in range(2):
+                each_z = sums[0][k] + 2.0 * sums[1][k]
+                if b:
+                    acc[k, r - 1] = acc[k, r - 1] + jnp.sum(each_z, axis=0)
+                else:
+                    rest = jnp.sum(each_z[Z - 2 :], axis=0)
+                    acc[k, r - 1] = acc[k, r - 1] + jnp.sum(each_z[: Z - 2], axis=0) + jnp.where(last, 0.0, rest)
+
+    def sums_of(b, low_z, rows):
+        strain(b, low_z, Z, rows)
+        collect(b, low_z, Z, rows)
+
+    turns_of(0, 2, Z)
+    products_of(0, 2, Z)
+    block = 3 * R * K
+    acc[...] = jnp.zeros(acc.shape, jnp.float32)
 
     @pl.when(first)
     def _():
-        ends(1, Z - 1, 4)
-        for r, pair_of in enumerate(phase(1, Z - 2, Z)):
-            for k in range(2):
-                acc[k, r] = jnp.sum(pair_of[k], axis=0)
+        drain(ZL, block * 4)
+        for c in range(3):
+            unpack(he[c], place(1, c, 1, Z - 2))
+            unpack(hz[0, c], place(1, c, 1, Z))
+        coarsen_block(1, Z - 2, 2)
+        coarsen_block(1, Z, 2)
+        for c in range(3):
+            for r in range(1, R + 1):
+                for i in range(2):
+                    put(0, c, r, i, get(1, c, r, Z + i, 1)[0])
+                    put(1, c, r, Z + 2 + i, get(0, c, r, 2 + i, 1)[0])
+        turns_of(1, Z - 2, 4)
+        products_of(1, Z - 1, 3)
+        local(1, Z - 2)
+        sums_of(1, Z - 2, range(2, R))
 
     @pl.when(ax > 0)
     def _():
-        acc[...] = jnp.zeros(acc.shape, jnp.float32)
+        drain(ZL, block * 2)
+        for c in range(3):
+            unpack(hz[0, c], place(0, c, 1, 0))
+        coarsen_block(0, 0, 2)
+        turns_of(0, 0, 2)
+        products_of(0, 1, 1)
+
+    @pl.when(ax < n_ax - 1)
+    def _():
+        drain(ZR, block * 2)
+        for c in range(3):
+            unpack(hz[1, c], place(0, c, 1, Z + 2))
+        coarsen_block(0, Z + 2, 2)
+        turns_of(0, Z + 2, 2)
+        products_of(0, Z + 2, 1)
+
+    local(0, 0)
+    sums_of(0, 0, range(2, R))
+
+    def rim_in(side, row):
+        line = 3 * K
+        pl.when(first)(lambda: drain(ROW + side, line * (Z + 4)))
+        pl.when(last)(lambda: drain(ROW + side, line * (Z + 1)))
+        pl.when((ax > 0) & (ax < n_ax - 1))(lambda: drain(ROW + side, line * (Z + 2)))
+        for c in range(3):
+            unpack(hr[side, c], place(0, c, row, -1))
+
+    def edge_out(row, end, to_rad):
+        group, slot = (2, EDGE + 1) if row == 1 else (1, EDGE)
+        send(hx.at[:, row], hx.at[:, end], group, slot, ax, to_rad)
+
+    def edge_rows(row):
+        for c in range(3):
+            hx[c, row] = flux[0, pair(c, 1), row - 1, 1 : Z + 1]
+        if row == 1:
+            pl.when(has_lo)(lambda: edge_out(1, R + 1, rad - 1))
+        else:
+            pl.when(has_hi)(lambda: edge_out(R, 0, rad + 1))
+
+    def finish(row, beyond):
+        strain(0, 0, Z, (row,))
+        pl.when(ax < n_ax - 1)(lambda: edge_rows(row))
+
+        @pl.when(first)
+        def _():
+            outside(1, Z - 2, beyond)
+            sums_of(1, Z - 2, (row,))
+
+        outside(0, 0, beyond)
+        collect(0, 0, Z, (row,))
+
+    pl.when(has_lo)(lambda: rim_in(0, 0))
+    coarsen_below(-1, Z + 4)
+
+    @pl.when(rad == 0)
+    def _():
+        axis_end(0, 1, Z + 2)
+        pl.when(first)(lambda: axis_end(1, Z - 1, 2))
+
+    finish(1, 0)
+    pl.when(has_hi)(lambda: rim_in(1, R + 1))
+    pl.when(rad == n_rad - 1)(wall_end)
+    finish(R, R + 1)
 
     sub_index = lax.broadcasted_iota(jnp.int32, (SUB, LANES), 0)
     lane_index = lax.broadcasted_iota(jnp.int32, (SUB, LANES), 1)
     mine = jnp.zeros((SUB, LANES), jnp.float32)
-    for r, pair_of in enumerate(phase(0, 0, Z)):
+    for r in range(R):
         for k in range(2):
-            whole = jnp.sum(pair_of[k][: Z - 2], axis=0)
-            rest = jnp.sum(pair_of[k][Z - 2 :], axis=0)
-            row = acc[k, r] + whole + jnp.where(last, 0.0, rest)
-            row = jnp.sum(row, axis=0, keepdims=True) * (2.0 ** -15, 2.0 ** -14)[k]
+            row = jnp.sum(acc[k, r], axis=0, keepdims=True) * (2.0 ** -15, 2.0 ** -14)[k]
             mine = jnp.where(sub_index == k * half + r, row, mine)
     mine = jnp.where((lane_index >= pad) & (lane_index < pad + wide), mine, 0.0)
     fold = LANES // 2
@@ -481,8 +532,8 @@
             for c in range(3):
                 unpack(hc[1, c], place(0, c, R + 1, Z + 2))
 
-        coarsen_below(0, Z + 2, 1)
-        ends(0, Z + 2, 1)
+        coarsen_below(Z + 2, 1)
+        pl.when(rad == 0)(lambda: axis_end(0, Z + 2, 1))
         for r in range(1, R + 1):
             grads = []
             for c in range(3):
@@ -495,12 +546,15 @@
                 ])
             terms, size = tensor(grads)
             for p in range(6):
-                flux[p, r - 1, Z : Z + 2] = size * terms[p]
+                flux[0, p, r - 1, Z : Z + 2] = size * terms[p]
+
+    @pl.when(last)
+    def _():
+        edge_rows(1)
+        edge_rows(R)
 
     for c in range(3):
-        hx[c, 1 : R + 1] = flux[pair(c, 1), :, 1 : Z + 1]
-    pl.when(has_hi)(lambda: send(hx.at[:, R], hx.at[:, 0], 1, EDGE, ax, rad + 1))
-    pl.when(has_lo)(lambda: send(hx.at[:, 1], hx.at[:, R + 1], 2, EDGE + 1, ax, rad - 1))
+        hx[c, 2:R] = flux[0, pair(c, 1), 1 : R - 1, 1 : Z + 1]
 
     @pl.when(rad == 0)
     def _():
@@ -521,12 +575,12 @@
             outer = get(0, c, r + 1, 2, Z) * get(0, 1, r + 1, 2, Z)
             inner = get(0, c, r - 1, 2, Z) * get(0, 1, r - 1, 2, Z)
             mid = get(0, c, r, 2, Z)
-            around = mid * get(0, 2, r, 2, Z)
-            change = axial[2:] - axial[:-2] + (outer - inner) + (up(around) - down(around))
+            spin = mid * get(0, 2, r, 2, Z)
+            change = axial[2:] - axial[:-2] + (outer - inner) + (up(spin) - down(spin))
             bases[c].append(mid - 0.5 * change)
-            turn = flux[pair(c, 2), r - 1, 1 : Z + 1]
+            turn = flux[0, pair(c, 2), r - 1, 1 : Z + 1]
             p = pair(c, 0)
-            turns[c].append(flux[p, r - 1, 2 : Z + 2] - flux[p, r - 1, 0:Z] + (up(turn) - down(turn)))
+            turns[c].append(flux[0, p, r - 1, 2 : Z + 2] - flux[0, p, r - 1, 0:Z] + (up(turn) - down(turn)))
 
     count = n_ax * Z * T
     sums_in(0, n_ax - 1)
@@ -614,16 +668,18 @@
             vmem(NRING * SUB, LANES),
             vmem(NRING, 2 * (MOSTSEG - 1).bit_length() + 1, SUB, LANES),
             vmem(3 * R * (Z + 10) * SUB, LANES),
-            vmem(2 * 3 * 2 * (Z + 4) * SUB, LANES),
+            vmem(3 * 2 * (Z + 4) * SUB, LANES),
             vmem(2, 3, 2 * R, T),
             vmem(3, 2 * R, T),
-            vmem(2, 3, Z + 2, T),
-            vmem(2, 3, 2, T),
+            vmem(2, 3, Z + 4, T),
             vmem(3, 2 * R, T),
             vmem(2, 3, 1, T),
             vmem(2, 3, R + 2, Z + 2, SUB, LANES),
             vmem(2, 6, R, Z, SUB, LANES),
-            vmem(6, R, Z + 2, SUB, LANES),
+            vmem(3, R, Z + 6, SUB, LANES),
+            vmem(3, R, Z + 6, SUB, LANES),
+            vmem(6, R, Z + 6, SUB, LANES),
+            vmem(2, 6, R, Z + 2, SUB, LANES),
             vmem(3, R + 2, Z, SUB, LANES),
             vmem(3 * R * Z * SUB, LANES),
             vmem(2, R, SUB, LANES),

time: 16 us -> 15.8 us (0.988); the launches traced: 15.9 us -> 15.5 us
  Pallas kernels: 15.2 us -> 14.9 us
    pallas_call x1, Pallas kernels: 15.2 us -> 14.9 us  [shards(): pl.pallas_call(functools.partial(kernel, n_ax, n_rad), out_shape=jax.Shap...]
where the time goes in v4:
time: 15.8 us; the launch traced here: 15.5 us
  Pallas kernels  14.9 us (94%)
  local copies, waits for them, and re-layouts  0.65 us (4%)
    pallas_call x1, Pallas kernels, shards(): pl.pallas_call(functools.partial(kernel, n_ax, n_rad), out_shape=jax.Shap...  14.9 us
    unnamed x1, local copies, waits for them, and re-layouts  0.65 us

profile of v4, /device:TPU:1, one launch (start us, length us, event | category | flops | bytes accessed | tf_op | source)
XLA Modules:
  0.0 15.5 jit_solution(1561947195557152507)
XLA Ops:
  0.0 14.9 %shard_map.28 = f32[3,3,3,768]{3,2,1,0:T(4,128)S(1)} custom-call(f32[3,3,3,768]{3,2,1,0:T(4,128)} %v_hbm.1, s32[3,768]{1,0:T(4,128)} %map_hbm.1), custom_call_target="tpu_custom_call" | custom-call | tf_op jit(solution)/shard_map/pallas_call | solution.py:660
  14.9 0.6 %copy.4 = f32[3,3,3,768]{3,2,1,0:T(4,128)} copy(f32[3,3,3,768]{3,2,1,0:T(4,128)S(1)} %shard_map.28) | data formatting | bytes 165888

commit v5 on v4

--- a/solution.py
+++ b/solution.py
@@ -105,7 +105,7 @@
 
 
 def kernel(n_ax, n_rad, v_hbm, map_hbm, out_ref, nat, map_ref, maps, masks, ext, rims, hz, he, hr, hl, hc, wsc,
-           lsc, around, slope, paired, flux, hx, res, acc, part, parts, edge_coef, spare, ready, sems):
+           lsc, around, slope, paired, flux, hx, res, acc, part, parts, spare, ready, sems):
     rad = lax.axis_index("rad")
     ax = lax.axis_index("ax")
     R, Z, T = nat.shape[1], nat.shape[2], nat.shape[3]
@@ -464,7 +464,8 @@
         collect(0, 0, Z, (row,))
 
     pl.when(has_lo)(lambda: rim_in(0, 0))
-    coarsen_below(-1, Z + 4)
+    coarsen_below(1, Z + 2)
+    pl.when(first)(lambda: coarsen_below(-1, 2))
 
     @pl.when(rad == 0)
     def _():
@@ -490,6 +491,7 @@
         fold //= 2
     group = lane_index // (LANES // SUB) == sub_index
     part[...] = jnp.sum(jnp.where(group, mine, 0.0), axis=0, keepdims=True)
+    parts[n_ax + ax] = part[...]
 
     def sums(side, i):
         peer = lax.rem(ax + i, n_ax)
@@ -583,43 +585,28 @@
             turns[c].append(flux[0, p, r - 1, 2 : Z + 2] - flux[0, p, r - 1, 0:Z] + (up(turn) - down(turn)))
 
     count = n_ax * Z * T
-    sums_in(0, n_ax - 1)
-
     def coefficients(total):
         total = jnp.broadcast_to(jnp.sum(jnp.where(group, total, 0.0), axis=1, keepdims=True), (SUB, LANES)) / count
         return 0.125 * (total / (roll(total, -half, 0) + EPSILON))
 
     def total_of(side):
-        start = first_of(side)
-        total = part[...] if start else jnp.zeros((1, LANES), jnp.float32)
-        if n_ax <= 16:
-            for i in range(start, n_ax):
-                total = total + parts[(1 + side) * n_ax + lax.rem(ax + i, n_ax)]
-            return total
-        return lax.fori_loop(
-            start, n_ax, lambda i, t: t + parts[(1 + side) * n_ax + lax.rem(ax + i, n_ax)], total)
-
-    coef = coefficients(total_of(0))
-
-    def beside(side, row):
-        sums_in(side, n_ax)
-        edge_coef[0 if side < 0 else 1] = jnp.broadcast_to(
-            coefficients(total_of(side))[row : row + 1], (SUB, LANES))
-
-    pl.when(has_lo)(lambda: beside(-1, R - 1))
-    pl.when(has_hi)(lambda: beside(1, 0))
-
-    @pl.when(rad == 0)
-    def _():
-        edge_coef[0] = jnp.broadcast_to(coef[0:1], (SUB, LANES))
-
-    @pl.when(rad == n_rad - 1)
-    def _():
-        edge_coef[1] = jnp.zeros((SUB, LANES), jnp.float32)
+        terms = parts[pl.ds((1 + side) * n_ax, n_ax)]
+        while terms.shape[0] % 2 == 0:
+            terms = terms[: terms.shape[0] // 2] + terms[terms.shape[0] // 2 :]
+        return jnp.sum(terms, axis=0)
+
+    def spread_row(x):
+        return jnp.broadcast_to(x, (SUB, LANES))
 
     pl.when(has_lo)(lambda: drain(EDGE, 3 * Z * SUB))
     pl.when(has_hi)(lambda: drain(EDGE + 1, 3 * Z * SUB))
-    by_row = [edge_coef[0]] + [jnp.broadcast_to(coef[r : r + 1], (SUB, LANES)) for r in range(R)] + [edge_coef[1]]
+    sums_in(0, n_ax - 1)
+    pl.when(has_lo)(lambda: sums_in(-1, n_ax))
+    pl.when(has_hi)(lambda: sums_in(1, n_ax))
+    lower, coef, higher = [coefficients(total_of(side)) for side in (-1, 0, 1)]
+    by_row = [spread_row(jnp.where(rad == 0, coef[0:1], lower[R - 1 : R]))]
+    by_row = by_row + [spread_row(coef[r : r + 1]) for r in range(R)]
+    by_row = by_row + [spread_row(jnp.where(rad == n_rad - 1, 0.0, higher[0:1]))]
     for c in range(3):
         for r in range(R):
             new = bases[c][r] + by_row[r + 1] * turns[c][r]
@@ -685,7 +672,6 @@
             vmem(2, R, SUB, LANES),
             vmem(1, LANES),
             vmem(3 * n_ax, 1, LANES),
-            vmem(2, SUB, LANES),
             vmem(3 * (R * 6 + Z) * SUB * (T // LANES) + 2 * n_ax, LANES),
             pltpu.SemaphoreType.REGULAR((len(stages(n_ax)),)),
             pltpu.SemaphoreType.DMA((SEMS,)),

time: 15.8 us -> 15.7 us (level)
  no operation moved by 1% of the time
where the time goes in v5:
time: 15.7 us; the launch traced here: 15.5 us
  Pallas kernels  14.9 us (95%)
  local copies, waits for them, and re-layouts  0.65 us (4%)
    pallas_call x1, Pallas kernels, shards(): pl.pallas_call(functools.partial(kernel, n_ax, n_rad), out_shape=jax.Shap...  14.9 us
    unnamed x1, local copies, waits for them, and re-layouts  0.65 us

profile of v5, /device:TPU:1, one launch (start us, length us, event | category | flops | bytes accessed | tf_op | source)
XLA Modules:
  0.0 15.5 jit_solution(671163504970323637)
XLA Ops:
  0.0 14.9 %shard_map.28 = f32[3,3,3,768]{3,2,1,0:T(4,128)S(1)} custom-call(f32[3,3,3,768]{3,2,1,0:T(4,128)} %v_hbm.1, s32[3,768]{1,0:T(4,128)} %map_hbm.1), custom_call_target="tpu_custom_call" | custom-call | tf_op jit(solution)/shard_map/pallas_call | solution.py:647
  14.9 0.6 %copy.4 = f32[3,3,3,768]{3,2,1,0:T(4,128)} copy(f32[3,3,3,768]{3,2,1,0:T(4,128)S(1)} %shard_map.28) | data formatting | bytes 165888

commit v6 on v5

--- a/solution.py
+++ b/solution.py
@@ -165,31 +165,34 @@
     row_sum = 4 - jnp.where(first, 2, 0) - jnp.where(ax == 1, 1, 0)
     pl.semaphore_wait(barrier, row_sum * (1 + beside_sum) + beside_sum)
 
-    def planes(first_z, count, dst, row, group, recv, to_ax):
+    def planes(src, first_z, count, dst, row, group, recv, to_ax):
         for r in range(R):
-            send(v_hbm.at[:, r, pl.ds(first_z, count)], dst.at[:, pl.ds(2 * r + row, count)], group, recv, to_ax, rad)
-
-    pl.when(last)(lambda: planes(Z - 2 - near, near, he, far, 0, ZL, right))
-    planes(Z - 2, 2, hz.at[0], 0, 0, ZL, right)
-    if far:
-        pl.when(second)(lambda: planes(Z - far, far, he, 0, 0, ZL, lax.rem(ax + 2, n_ax)))
-    pl.when(ax > 0)(lambda: planes(0, 2, hz.at[1], 0, 0, ZR, left))
-
-    def rim(side, group, row, to_rad):
-        send(v_hbm.at[:, row, pl.ds(Z - 1, 1)], hr.at[side, :, pl.ds(2, 1)], group, ROW + side, right, to_rad)
-
-        @pl.when(last)
-        def _():
-            send(v_hbm.at[:, row, pl.ds(Z - 3, 2)], hr.at[side, :, pl.ds(0, 2)], group, ROW + side, right, to_rad)
+            send(src.at[:, r, pl.ds(first_z, count)], dst.at[:, pl.ds(2 * r + row, count)], group, recv, to_ax, rad)
+
+    def rim(src, at_end, side, group, row, to_rad):
+        send(src.at[:, row, pl.ds(Z - 1, 1)], hr.at[side, :, pl.ds(2, 1)], group, ROW + side, right, to_rad)
+        if at_end:
+            send(src.at[:, row, pl.ds(Z - 3, 2)], hr.at[side, :, pl.ds(0, 2)], group, ROW + side, right, to_rad)
 
         @pl.when(ax > 0)
         def _():
-            send(v_hbm.at[:, row, pl.ds(0, 1)], hr.at[side, :, pl.ds(Z + 3, 1)], group, ROW + side, left, to_rad)
-
-        send(v_hbm.at[:, row], hr.at[side, :, pl.ds(3, Z)], group, ROW + side, ax, to_rad)
-
-    pl.when(has_hi)(lambda: rim(0, 1, R - 1, rad + 1))
-    pl.when(has_lo)(lambda: rim(1, 2, 0, rad - 1))
+            send(src.at[:, row, pl.ds(0, 1)], hr.at[side, :, pl.ds(Z + 3, 1)], group, ROW + side, left, to_rad)
+
+        send(src.at[:, row], hr.at[side, :, pl.ds(3, Z)], group, ROW + side, ax, to_rad)
+
+    def halos(src, at_end):
+        if at_end:
+            planes(src, Z - 2 - near, near, he, far, 0, ZL, right)
+        planes(src, Z - 2, 2, hz.at[0], 0, 0, ZL, right)
+        if far and not at_end:
+            pl.when(second)(lambda: planes(src, Z - far, far, he, 0, 0, ZL, lax.rem(ax + 2, n_ax)))
+        pl.when(ax > 0)(lambda: planes(src, 0, 2, hz.at[1], 0, 0, ZR, left))
+        pl.when(has_hi)(lambda: rim(src, at_end, 0, 1, R - 1, rad + 1))
+        pl.when(has_lo)(lambda: rim(src, at_end, 1, 2, 0, rad - 1))
+
+    pl.when(last)(lambda: halos(v_hbm, True))
+    fetch.wait()
+    pl.when(ax < n_ax - 1)(lambda: halos(nat, False))
     pl.when(ax > 1)(lambda: tell(0))
 
     def row_of(b, c, r, i):
@@ -281,7 +284,6 @@
                 masks[ring, S + k] = (roll(label, -d, 1) == label).astype(jnp.float32)
             masks[ring, 2 * S] = 1.0 / spread(ring, jnp.ones((SUB, LANES), jnp.float32))
 
-    fetch.wait()
     for c in range(3):
         for r in range(R):
             unpack(nat[c, r], place(0, c, r + 1, 2))
@@ -321,9 +323,9 @@
 
     @pl.when(first)
     def _():
-        planes(0, 2, hl, 0, 0, LATE, left)
-        pl.when(has_hi)(lambda: send(v_hbm.at[:, R - 1, pl.ds(0, 1)], hc.at[0], 1, LATE + 1, left, rad + 1))
-        pl.when(has_lo)(lambda: send(v_hbm.at[:, 0, pl.ds(0, 1)], hc.at[1], 2, LATE + 2, left, rad - 1))
+        planes(nat, 0, 2, hl, 0, 0, LATE, left)
+        pl.when(has_hi)(lambda: send(nat.at[:, R - 1, pl.ds(0, 1)], hc.at[0], 1, LATE + 1, left, rad + 1))
+        pl.when(has_lo)(lambda: send(nat.at[:, 0, pl.ds(0, 1)], hc.at[1], 2, LATE + 2, left, rad - 1))
 
     def axis_end(b, first_i, count):
         for c in range(3):

time: 15.7 us -> 15.6 us (level)
  no operation moved by 1% of the time
where the time goes in v6:
time: 15.6 us; the launch traced here: 15.5 us
  Pallas kernels  14.8 us (95%)
  local copies, waits for them, and re-layouts  0.65 us (4%)
    pallas_call x1, Pallas kernels, shards(): pl.pallas_call(functools.partial(kernel, n_ax, n_rad), out_shape=jax.Shap...  14.8 us
    unnamed x1, local copies, waits for them, and re-layouts  0.65 us

profile of v6, /device:TPU:1, one launch (start us, length us, event | category | flops | bytes accessed | tf_op | source)
XLA Modules:
  0.0 15.5 jit_solution(14537203064256907011)
XLA Ops:
  0.0 14.8 %shard_map.28 = f32[3,3,3,768]{3,2,1,0:T(4,128)S(1)} custom-call(f32[3,3,3,768]{3,2,1,0:T(4,128)} %v_hbm.1, s32[3,768]{1,0:T(4,128)} %map_hbm.1), custom_call_target="tpu_custom_call" | custom-call | tf_op jit(solution)/shard_map/pallas_call | solution.py:649
  14.9 0.6 %copy.4 = f32[3,3,3,768]{3,2,1,0:T(4,128)} copy(f32[3,3,3,768]{3,2,1,0:T(4,128)S(1)} %shard_map.28) | data formatting | bytes 165888

commit v7 on v6

--- a/solution.py
+++ b/solution.py
@@ -105,7 +105,7 @@
 
 
 def kernel(n_ax, n_rad, v_hbm, map_hbm, out_ref, nat, map_ref, maps, masks, ext, rims, hz, he, hr, hl, hc, wsc,
-           lsc, around, slope, paired, flux, hx, res, acc, part, parts, spare, ready, sems):
+           lsc, around, slope, paired, flux, hx, res, flat, acc, part, parts, spare, ready, sems):
     rad = lax.axis_index("rad")
     ax = lax.axis_index("ax")
     R, Z, T = nat.shape[1], nat.shape[2], nat.shape[3]
@@ -572,7 +572,17 @@
             for z in range(Z):
                 hx[c, R + 1, z] = jnp.zeros((SUB, LANES), jnp.float32)
 
-    bases, turns = [[], [], []], [[], [], []]
+    def lay(slot, x):
+        base = slot * Z * SUB
+        for z in range(Z):
+            res[base + z * SUB : base + (z + 1) * SUB, :] = x[z]
+        pieces = [res[pl.ds(base + s, Z, stride=SUB), :] for s in range(SUB)]
+        for k, tile in enumerate(joined(pieces, wide, pad)):
+            flat[slot, :, k * LANES : (k + 1) * LANES] = tile
+
+    def slot_of(kind, c, r):
+        return (kind * 3 + c) * (R + 2) + r
+
     for r in range(1, R + 1):
         for c in range(3):
             axial = get(0, c, r, 1, Z + 2) * get(0, 0, r, 1, Z + 2)
@@ -581,10 +591,12 @@
             mid = get(0, c, r, 2, Z)
             spin = mid * get(0, 2, r, 2, Z)
             change = axial[2:] - axial[:-2] + (outer - inner) + (up(spin) - down(spin))
-            bases[c].append(mid - 0.5 * change)
+            lay(slot_of(0, c, r), mid - 0.5 * change)
             turn = flux[0, pair(c, 2), r - 1, 1 : Z + 1]
             p = pair(c, 0)
-            turns[c].append(flux[0, p, r - 1, 2 : Z + 2] - flux[0, p, r - 1, 0:Z] + (up(turn) - down(turn)))
+            along = flux[0, p, r - 1, 2 : Z + 2] - flux[0, p, r - 1, 0:Z]
+            lay(slot_of(1, c, r), along + (up(turn) - down(turn)))
+            lay(slot_of(2, c, r), hx[c, r])
 
     count = n_ax * Z * T
     def coefficients(total):
@@ -598,10 +610,13 @@
         return jnp.sum(terms, axis=0)
 
     def spread_row(x):
-        return jnp.broadcast_to(x, (SUB, LANES))
+        return jnp.broadcast_to(x, (Z, LANES))
 
     pl.when(has_lo)(lambda: drain(EDGE, 3 * Z * SUB))
     pl.when(has_hi)(lambda: drain(EDGE + 1, 3 * Z * SUB))
+    for c in range(3):
+        for r in (0, R + 1):
+            lay(slot_of(2, c, r), hx[c, r])
     sums_in(0, n_ax - 1)
     pl.when(has_lo)(lambda: sums_in(-1, n_ax))
     pl.when(has_hi)(lambda: sums_in(1, n_ax))
@@ -610,18 +625,12 @@
     by_row = by_row + [spread_row(coef[r : r + 1]) for r in range(R)]
     by_row = by_row + [spread_row(jnp.where(rad == n_rad - 1, 0.0, higher[0:1]))]
     for c in range(3):
-        for r in range(R):
-            new = bases[c][r] + by_row[r + 1] * turns[c][r]
-            new = new + (by_row[r + 2] * hx[c, r + 2] - by_row[r] * hx[c, r])
-            for z in range(Z):
-                row = ((c * R + r) * Z + z) * SUB
-                res[row : row + SUB, :] = new[z]
-    for c in range(3):
-        for r in range(R):
-            base = (c * R + r) * Z * SUB
-            pieces = [res[pl.ds(base + s, Z, stride=SUB), :] for s in range(SUB)]
-            for k, tile in enumerate(joined(pieces, wide, pad)):
-                out_ref[c, r, :, k * LANES : (k + 1) * LANES] = tile
+        for r in range(1, R + 1):
+            for k in range(K):
+                lanes = slice(k * LANES, (k + 1) * LANES)
+                base, turn, outer, inner = [
+                    flat[slot_of(*at), :, lanes] for at in ((0, c, r), (1, c, r), (2, c, r + 1), (2, c, r - 1))]
+                out_ref[c, r - 1, :, lanes] = base + by_row[r] * turn + (by_row[r + 1] * outer - by_row[r - 1] * inner)
 
     middle = (ax > 0) & (ax < n_ax - 2)
 
@@ -670,7 +679,8 @@
             vmem(6, R, Z + 6, SUB, LANES),
             vmem(2, 6, R, Z + 2, SUB, LANES),
             vmem(3, R + 2, Z, SUB, LANES),
-            vmem(3 * R * Z * SUB, LANES),
+            vmem(9 * (R + 2) * Z * SUB, LANES),
+            vmem(9 * (R + 2), Z, T),
             vmem(2, R, SUB, LANES),
             vmem(1, LANES),
             vmem(3 * n_ax, 1, LANES),

time: 15.6 us -> 15.5 us (level)
  no operation moved by 1% of the time
where the time goes in v7:
time: 15.5 us; the launch traced here: 15.4 us
  Pallas kernels  14.7 us (95%)
  local copies, waits for them, and re-layouts  0.65 us (4%)
    pallas_call x1, Pallas kernels, shards(): pl.pallas_call(functools.partial(kernel, n_ax, n_rad), out_shape=jax.Shap...  14.7 us
    unnamed x1, local copies, waits for them, and re-layouts  0.65 us

profile of v7, /device:TPU:1, one launch (start us, length us, event | category | flops | bytes accessed | tf_op | source)
XLA Modules:
  0.0 15.4 jit_solution(14213573952934497034)
XLA Ops:
  0.0 14.7 %shard_map.28 = f32[3,3,3,768]{3,2,1,0:T(4,128)S(1)} custom-call(f32[3,3,3,768]{3,2,1,0:T(4,128)} %v_hbm.1, s32[3,768]{1,0:T(4,128)} %map_hbm.1), custom_call_target="tpu_custom_call" | custom-call | tf_op jit(solution)/shard_map/pallas_call | solution.py:658
  14.7 0.6 %copy.4 = f32[3,3,3,768]{3,2,1,0:T(4,128)} copy(f32[3,3,3,768]{3,2,1,0:T(4,128)S(1)} %shard_map.28) | data formatting | bytes 165888

commit v8 on v7

--- a/solution.py
+++ b/solution.py
@@ -632,20 +632,18 @@
                     flat[slot_of(*at), :, lanes] for at in ((0, c, r), (1, c, r), (2, c, r + 1), (2, c, r - 1))]
                 out_ref[c, r - 1, :, lanes] = base + by_row[r] * turn + (by_row[r + 1] * outer - by_row[r - 1] * inner)
 
-    middle = (ax > 0) & (ax < n_ax - 2)
-
-    def sent(group, usual, for_first, for_last, for_second):
-        pl.when(middle)(lambda: drain(SEND + group, usual))
-        pl.when(first)(lambda: drain(SEND + group, for_first))
-        pl.when(last)(lambda: drain(SEND + group, for_last))
-        pl.when(second)(lambda: drain(SEND + group, for_second))
-
     line, total = 3 * K, n_ax - 1
-    sent(0, 4 * block + total, 4 * block + total, (4 + near) * block + total, (4 + far) * block + total)
-    total = 3 * Z * SUB + n_ax
-    usual, more = line * (Z + 2) + total, line * (Z + 4) + total
-    pl.when(has_hi)(lambda: sent(1, usual, usual, more, usual))
-    pl.when(has_lo)(lambda: sent(2, usual, usual, more, usual))
+    pl.when(ax < n_ax - 2)(lambda: drain(SEND, 4 * block + total))
+    pl.when(last)(lambda: drain(SEND, (4 + near) * block + total))
+    pl.when(second)(lambda: drain(SEND, (4 + far) * block + total))
+
+    def sent(group):
+        usual = line * (Z + 2) + 3 * Z * SUB + n_ax
+        pl.when(ax < n_ax - 1)(lambda: drain(SEND + group, usual))
+        pl.when(last)(lambda: drain(SEND + group, usual + 2 * line))
+
+    pl.when(has_hi)(lambda: sent(1))
+    pl.when(has_lo)(lambda: sent(2))
 
 
 def shards(n_ax, n_rad, velocity, cycle_map):

time: 15.5 us -> 15.5 us (level)
  no operation moved by 1% of the time
where the time goes in v8:
time: 15.5 us; the launch traced here: 15.4 us
  Pallas kernels  14.7 us (95%)
  local copies, waits for them, and re-layouts  0.65 us (4%)
    pallas_call x1, Pallas kernels, shards(): pl.pallas_call(functools.partial(kernel, n_ax, n_rad), out_shape=jax.Shap...  14.7 us
    unnamed x1, local copies, waits for them, and re-layouts  0.65 us

profile of v8, /device:TPU:1, one launch (start us, length us, event | category | flops | bytes accessed | tf_op | source)
XLA Modules:
  0.0 15.4 jit_solution(9264920742670290826)
XLA Ops:
  0.0 14.7 %shard_map.28 = f32[3,3,3,768]{3,2,1,0:T(4,128)S(1)} custom-call(f32[3,3,3,768]{3,2,1,0:T(4,128)} %v_hbm.1, s32[3,768]{1,0:T(4,128)} %map_hbm.1), custom_call_target="tpu_custom_call" | custom-call | tf_op jit(solution)/shard_map/pallas_call | solution.py:656
  14.7 0.6 %copy.4 = f32[3,3,3,768]{3,2,1,0:T(4,128)} copy(f32[3,3,3,768]{3,2,1,0:T(4,128)S(1)} %shard_map.28) | data formatting | bytes 165888
